TPU v7x, 32 devices: a whole 2x2x4 slice. The times are simulated.
32 devices in a mesh: sensor: 16 (over z, x, core), batch: 2 (over y).
Axes of the slice: x: 2, y: 2, z: 4, core: 2. Of those that a mesh axis runs over, the one named last changes fastest.
Arguments:
- pixels: bfloat16 [64, 1024, 832], P(('sensor', 'batch')), may hold values from -6 to 6
- visible: int32 [64, 256], P(('sensor', 'batch')), may hold values from 0 to 1023, as said below
- chip_size: int32 [64], P(('sensor', 'batch')), may hold values from 256 to 1024, as said below
- sensor_id: int32 [64], P(('sensor', 'batch')), may hold values from 0 to 3, as said below
- band_count: int32 [4], replicated, may hold values from 3 to 13
- wavelengths: float32 [4, 13], replicated, may hold values from 0.4 to 2.4
- time_place: float32 [64, 8], P(('sensor', 'batch')), may hold values from -1 to 1
- cls_token: float32 [768], replicated, may hold values from -5 to 5
- w_meta: bfloat16 [8, 768], replicated, may hold values from -2 to 2
- w_wave1: bfloat16 [128, 128], replicated, may hold values from -0.5 to 0.5
- wave1_bias: float32 [128], replicated, may hold values from -3 to 3
- w_wave2: bfloat16 [49152, 128], P(('sensor', 'batch')), may hold values from -0.02734375 to 0.02734375
- patch_bias: float32 [768], replicated, may hold values from -2 to 2
- ln1_gain: float32 [768], replicated, may hold values from 0.5 to 1.5
- ln1_bias: float32 [768], replicated, may hold values from -2 to 2
- w_qkv: bfloat16 [768, 2304], P(('sensor', 'batch')), may hold values from -0.21875 to 0.21875
- w_out: bfloat16 [768, 768], P(('sensor', 'batch')), may hold values from -1.75 to 1.75
- out_bias: float32 [768], replicated, may hold values from -2 to 2
- ln2_gain: float32 [768], replicated, may hold values from 0.5 to 1.5
- ln2_bias: float32 [768], replicated, may hold values from -2 to 2
- w_fc1: bfloat16 [768, 3072], P(('sensor', 'batch')), may hold values from -0.21875 to 0.21875
- fc1_bias: float32 [3072], replicated, may hold values from -3 to 3
- w_fc2: bfloat16 [3072, 768], P(('sensor', 'batch')), may hold values from -0.109375 to 0.109375
- fc2_bias: float32 [768], replicated, may hold values from -2 to 2
- cotangent: bfloat16 [64, 258, 768], P(('sensor', 'batch')), may hold values from -6 to 6
Outputs:
- mixed: bfloat16 [64, 258, 768], P(('sensor', 'batch'))
- grad_pixels: float32 [64, 1024, 832], P(('sensor', 'batch'))
- grad_time_place: float32 [64, 8], P(('sensor', 'batch'))
- grad_cls: float32 [768], replicated
- grad_w_meta: float32 [8, 768], replicated
- grad_w_wave1: float32 [128, 128], replicated
- grad_wave1_bias: float32 [128], replicated
- grad_w_wave2: float32 [49152, 128], P(('sensor', 'batch'))
- grad_patch_bias: float32 [768], replicated
- grad_ln1_gain: float32 [768], replicated
- grad_ln1_bias: float32 [768], replicated
- grad_w_qkv: float32 [768, 2304], P(('sensor', 'batch'))
- grad_w_out: float32 [768, 768], P(('sensor', 'batch'))
- grad_out_bias: float32 [768], replicated
- grad_ln2_gain: float32 [768], replicated
- grad_ln2_bias: float32 [768], replicated
- grad_w_fc1: float32 [768, 3072], P(('sensor', 'batch'))
- grad_fc1_bias: float32 [3072], replicated
- grad_w_fc2: float32 [3072, 768], P(('sensor', 'batch'))
- grad_fc2_bias: float32 [768], replicated
Inputs may be any that keep to these rules, and one draw needn't show every extreme that they name: `chip_size`: each is 1024 or 256. `visible`: each chip's entries are distinct patches below its chip_size; for a chip of 256 patches only the first 64 entries are read. `sensor_id`: each sensor has exactly 16 chips, anywhere among the chips.
All inputs are finite; a program needn't handle non-finite values.
Results may differ from a plain program's by a relative error of at most 0.02.
Values may be sent and summed in bfloat16 or wider, within the bound.
No kernel may reach another device: no remote copies, remote signals or barrier semaphores. Data moves between devices by JAX's collectives and lax.ppermute only.
A program may use at most 256 MiB of HBM per device.

v0:
```python
import math

import jax
import jax.numpy as jnp
from jax import lax
from jax.sharding import PartitionSpec as P

D = 768
HEADS = 12
HYPER = 128
SIDE = 32
MAXP = 1024


PRECISE = lax.Precision.HIGHEST
EPSILON = 1e-05
MASKED = -1e30


def wave_code(wavelengths):
    halfwidth = HYPER // 2
    freqs = 10000.0 ** (-jnp.arange(halfwidth, dtype=jnp.float32) / halfwidth)
    angles = (wavelengths * 1000.0)[:, :, None] * freqs
    return jnp.concatenate([jnp.sin(angles), jnp.cos(angles)], axis=-1)


def place_code(visible, chip_size):
    side_len = jnp.where(chip_size == MAXP, SIDE, SIDE // 2).astype(jnp.int32)
    row_pos = (visible // side_len[:, None]).astype(jnp.float32)
    col_pos = (visible % side_len[:, None]).astype(jnp.float32)
    quarter = D // 4
    freqs = 10000.0 ** (-jnp.arange(quarter, dtype=jnp.float32) / quarter)
    row_ang = row_pos[..., None] * freqs
    col_ang = col_pos[..., None] * freqs
    return jnp.concatenate(
        [jnp.sin(row_ang), jnp.cos(row_ang), jnp.sin(col_ang), jnp.cos(col_ang)], axis=-1
    )


def norm_forward(values, gain, offset):
    center = values - jnp.mean(values, axis=-1, keepdims=True)
    inv_std = lax.rsqrt(jnp.mean(center * center, axis=-1, keepdims=True) + EPSILON)
    normed = center * inv_std
    return (normed * gain + offset, normed, inv_std)


def norm_backward(upstream, normed, inv_std, gain):
    scaled = upstream * gain
    back = inv_std * (
        scaled
        - jnp.mean(scaled, axis=-1, keepdims=True)
        - normed * jnp.mean(scaled * normed, axis=-1, keepdims=True)
    )
    return (back, jnp.sum(upstream * normed, axis=0), jnp.sum(upstream, axis=0))


def gelu_parts(values):
    cumul = 0.5 * (1.0 + lax.erf(values * 0.5**0.5))
    density = jnp.exp(-0.5 * values * values) * (2.0 * math.pi) ** (-0.5)
    return (values * cumul, cumul + values * density)


def masked_scores(query, keyed, allowed, scale):
    scores = jnp.einsum("qhe,khe->hqk", query, keyed, preferred_element_type=jnp.float32) * scale
    return jnp.where(allowed[None], scores, MASKED)


def attend(query, keyed, valued, allowed, scale):
    scores = masked_scores(query, keyed, allowed, scale)
    top_s = jnp.max(scores, axis=-1, keepdims=True)
    expd = jnp.exp(scores - top_s)
    denom = jnp.sum(expd, axis=-1, keepdims=True)
    probs = (expd / denom).astype(jnp.bfloat16)
    result = jnp.einsum("hqk,khe->qhe", probs, valued, preferred_element_type=jnp.float32)
    return (result.astype(jnp.bfloat16), (top_s + jnp.log(denom))[..., 0])


def attend_back(query, keyed, valued, allowed, log_total, upstream, scale):
    scores = masked_scores(query, keyed, allowed, scale)
    probs = jnp.exp(scores - log_total[..., None])
    grad_val = jnp.einsum(
        "hqk,qhe->khe", probs.astype(jnp.bfloat16), upstream, preferred_element_type=jnp.float32
    )
    grad_prob = jnp.einsum("qhe,khe->hqk", upstream, valued, preferred_element_type=jnp.float32)
    grad_score = (probs * (grad_prob - jnp.sum(probs * grad_prob, axis=-1, keepdims=True))).astype(
        jnp.bfloat16
    )
    grad_query = (
        jnp.einsum("hqk,khe->qhe", grad_score, keyed, preferred_element_type=jnp.float32) * scale
    )
    grad_key = (
        jnp.einsum("hqk,qhe->khe", grad_score, query, preferred_element_type=jnp.float32) * scale
    )
    return (
        grad_query.astype(jnp.bfloat16),
        grad_key.astype(jnp.bfloat16),
        grad_val.astype(jnp.bfloat16),
    )


def split_dot(form, exact, other):
    upper = exact.astype(jnp.bfloat16)
    lower = (exact - upper.astype(jnp.float32)).astype(jnp.bfloat16)
    first_term = jnp.einsum(form, upper, other, preferred_element_type=jnp.float32)
    return first_term + jnp.einsum(form, lower, other, preferred_element_type=jnp.float32)


def local(
    pixels,
    visible,
    chip_size,
    sensor_id,
    band_count,
    wavelengths,
    time_place,
    cls_token,
    w_meta,
    w_wave1,
    wave1_bias,
    w_wave2,
    patch_bias,
    ln1_gain,
    ln1_bias,
    w_qkv,
    w_out,
    out_bias,
    ln2_gain,
    ln2_bias,
    w_fc1,
    fc1_bias,
    w_fc2,
    fc2_bias,
    cotangent,
):
    single = jnp.float32
    half_t = jnp.bfloat16
    chips = pixels.shape[0]
    sensors, bands = wavelengths.shape
    length = cotangent.shape[1]
    width = cotangent.shape[2]
    head_dim = width // HEADS
    scale = head_dim ** (-0.5)
    rows_all = chips * length
    code = wave_code(wavelengths).reshape(sensors * bands, -1)
    band_mask = (jnp.arange(bands)[None, :] < band_count[:, None]).astype(single).reshape(-1, 1)
    pre_act = jnp.dot(code, w_wave1.astype(single), precision=PRECISE) + wave1_bias
    activ, activ_slope = gelu_parts(pre_act)
    embed_low = (activ * band_mask).astype(half_t)
    generator = lax.all_gather(w_wave2, ("sensor", "batch"), axis=0, tiled=True)
    kernel_flat = jnp.einsum(
        "rh,ch->rc", embed_low, generator, preferred_element_type=single
    ).astype(half_t)
    kernel = kernel_flat.reshape(sensors, -1, width)
    proj_qkv, proj_out, proj_up, proj_down = (
        lax.all_gather(w_qkv, ("sensor", "batch"), axis=0, tiled=True),
        lax.all_gather(w_out, ("sensor", "batch"), axis=0, tiled=True),
        lax.all_gather(w_fc1, ("sensor", "batch"), axis=0, tiled=True),
        lax.all_gather(w_fc2, ("sensor", "batch"), axis=0, tiled=True),
    )
    patches = jnp.take_along_axis(pixels, visible[:, :, None], axis=1)
    kern_chip = kernel[sensor_id]
    embedded = jnp.einsum("cvp,cpd->cvd", patches, kern_chip, preferred_element_type=single)
    tokens = embedded + place_code(visible, chip_size) + patch_bias
    meta_tok = jnp.dot(time_place, w_meta.astype(single), precision=PRECISE)
    first = jnp.broadcast_to(cls_token, (chips, 1, width))
    start = jnp.concatenate([first, meta_tok[:, None, :], tokens], axis=1).reshape(rows_all, width)
    valid = jnp.arange(length)[None, :] < (2 + chip_size // 4)[:, None]
    keep_rows = valid.reshape(rows_all, 1).astype(single)
    normed_one, hat_one, inv_one = norm_forward(start, ln1_gain, ln1_bias)
    normed_one = normed_one.astype(half_t)
    joined = jnp.dot(normed_one, proj_qkv, preferred_element_type=single).astype(half_t)
    per_block = math.gcd(chips, max(1, 600 // length))
    num_blocks = chips // per_block
    span = per_block * length
    query = joined[:, :width].reshape(num_blocks, span, HEADS, head_dim)
    keyed = joined[:, width : 2 * width].reshape(num_blocks, span, HEADS, head_dim)
    valued = joined[:, 2 * width :].reshape(num_blocks, span, HEADS, head_dim)
    valid_blocks = valid.reshape(num_blocks, span)
    owner = jnp.arange(span) // length

    def allowed_of(valid_row):
        return (owner[:, None] == owner[None, :]) & valid_row[None, :]

    def forward_block(inputs):
        q_blk, k_blk, v_blk, m_blk = inputs
        return attend(q_blk, k_blk, v_blk, allowed_of(m_blk), scale)

    attn, log_total = lax.map(forward_block, (query, keyed, valued, valid_blocks))
    attn = attn.reshape(rows_all, width)
    middle = start + jnp.dot(attn, proj_out, preferred_element_type=single) + out_bias
    normed_two, hat_two, inv_two = norm_forward(middle, ln2_gain, ln2_bias)
    normed_two = normed_two.astype(half_t)
    pre_up = jnp.dot(normed_two, proj_up, preferred_element_type=single) + fc1_bias
    hidden_f, hidden_slope = gelu_parts(pre_up)
    hidden = hidden_f.astype(half_t)
    final = middle + jnp.dot(hidden, proj_down, preferred_element_type=single) + fc2_bias
    mixed = (final * keep_rows).astype(half_t).reshape(chips, length, width)
    proj_qkv, proj_out, proj_up, proj_down = (
        lax.all_gather(w_qkv, ("sensor", "batch"), axis=0, tiled=True),
        lax.all_gather(w_out, ("sensor", "batch"), axis=0, tiled=True),
        lax.all_gather(w_fc1, ("sensor", "batch"), axis=0, tiled=True),
        lax.all_gather(w_fc2, ("sensor", "batch"), axis=0, tiled=True),
    )
    grad_final = cotangent.reshape(rows_all, width).astype(single) * keep_rows
    grad_branch = grad_final.astype(half_t)
    g_fc2_bias = jnp.sum(grad_branch.astype(single), axis=0)
    g_down = jnp.einsum("rf,rd->fd", hidden, grad_branch, preferred_element_type=single)
    grad_hidden = jnp.einsum("rd,fd->rf", grad_branch, proj_down, preferred_element_type=single)
    grad_up = (grad_hidden * hidden_slope).astype(half_t)
    g_fc1_bias = jnp.sum(grad_up.astype(single), axis=0)
    g_up = jnp.einsum("rd,rf->df", normed_two, grad_up, preferred_element_type=single)
    grad_norm_two = jnp.einsum("rf,df->rd", grad_up, proj_up, preferred_element_type=single)
    back_two, g_ln2_gain, g_ln2_bias = norm_backward(grad_norm_two, hat_two, inv_two, ln2_gain)
    grad_middle = grad_final + back_two
    grad_attn_out = grad_middle.astype(half_t)
    g_out_bias = jnp.sum(grad_attn_out.astype(single), axis=0)
    g_out = jnp.einsum("rd,re->de", attn, grad_attn_out, preferred_element_type=single)
    grad_attn = jnp.einsum(
        "re,de->rd", grad_attn_out, proj_out, preferred_element_type=single
    ).astype(half_t)

    def backward_block(inputs):
        q_blk, k_blk, v_blk, m_blk, lse_blk, up_blk = inputs
        return attend_back(q_blk, k_blk, v_blk, allowed_of(m_blk), lse_blk, up_blk, scale)

    grad_q, grad_k, grad_v = lax.map(
        backward_block,
        (
            query,
            keyed,
            valued,
            valid_blocks,
            log_total,
            grad_attn.reshape(num_blocks, span, HEADS, head_dim),
        ),
    )
    grad_joined = jnp.concatenate(
        [
            grad_q.reshape(rows_all, width),
            grad_k.reshape(rows_all, width),
            grad_v.reshape(rows_all, width),
        ],
        axis=1,
    )
    g_qkv = jnp.einsum("rd,re->de", normed_one, grad_joined, preferred_element_type=single)
    grad_norm_one = jnp.einsum("re,de->rd", grad_joined, proj_qkv, preferred_element_type=single)
    back_one, g_ln1_gain, g_ln1_bias = norm_backward(grad_norm_one, hat_one, inv_one, ln1_gain)
    grad_start = (grad_middle + back_one).reshape(chips, length, width)
    g_cls = jnp.sum(grad_start[:, 0, :], axis=0)
    grad_meta = grad_start[:, 1, :]
    g_w_meta = jnp.einsum("cm,cd->md", time_place, grad_meta, precision=PRECISE)
    g_time_place = jnp.einsum("cd,md->cm", grad_meta, w_meta.astype(single), precision=PRECISE)
    grad_tokens = grad_start[:, 2:, :]
    g_patch_bias = jnp.sum(grad_tokens, axis=(0, 1))
    grad_embedded = grad_tokens.astype(half_t)
    grad_patches = jnp.einsum(
        "cvd,cpd->cvp", grad_embedded, kern_chip, preferred_element_type=single
    )
    chip_rows = jnp.arange(chips)[:, None]
    g_pixels = jnp.zeros(pixels.shape, single).at[chip_rows, visible].add(grad_patches)
    kern_terms = jnp.einsum("cvp,cvd->cpd", patches, grad_embedded, preferred_element_type=single)
    selector = (sensor_id[:, None] == jnp.arange(sensors)[None, :]).astype(half_t)
    grad_kernel = split_dot("cpd,cs->spd", kern_terms, selector).reshape(sensors * bands, -1)
    g_wave2 = lax.psum_scatter(
        split_dot("rc,rh->ch", grad_kernel, embed_low),
        ("sensor", "batch"),
        scatter_dimension=0,
        tiled=True,
    )
    grad_embed = split_dot("rc,ch->rh", grad_kernel, generator)
    grad_pre = grad_embed * band_mask * activ_slope
    g_wave1 = jnp.einsum("rh,rk->hk", code, grad_pre, precision=PRECISE)
    g_wave1_bias = jnp.sum(grad_pre, axis=0)
    summed = lax.psum(
        (
            g_cls,
            g_w_meta,
            g_wave1,
            g_wave1_bias,
            g_patch_bias,
            g_ln1_gain,
            g_ln1_bias,
            g_out_bias,
            g_ln2_gain,
            g_ln2_bias,
            g_fc1_bias,
            g_fc2_bias,
        ),
        ("sensor", "batch"),
    )
    shared = (
        lax.psum_scatter(g_qkv, ("sensor", "batch"), scatter_dimension=0, tiled=True),
        lax.psum_scatter(g_out, ("sensor", "batch"), scatter_dimension=0, tiled=True),
        lax.psum_scatter(g_up, ("sensor", "batch"), scatter_dimension=0, tiled=True),
        lax.psum_scatter(g_down, ("sensor", "batch"), scatter_dimension=0, tiled=True),
    )
    return (
        mixed,
        g_pixels,
        g_time_place,
        summed[0],
        summed[1],
        summed[2],
        summed[3],
        g_wave2,
        summed[4],
        summed[5],
        summed[6],
        shared[0],
        shared[1],
        summed[7],
        summed[8],
        summed[9],
        shared[2],
        summed[10],
        shared[3],
        summed[11],
    )


def solution(mesh):
    return jax.shard_map(
        local,
        mesh=mesh,
        in_specs=(
            P(("sensor", "batch"), None, None),
            P(("sensor", "batch"), None),
            P(("sensor", "batch")),
            P(("sensor", "batch")),
            P(),
            P(),
            P(("sensor", "batch"), None),
            P(),
            P(),
            P(),
            P(),
            P(("sensor", "batch"), None),
            P(),
            P(),
            P(),
            P(("sensor", "batch"), None),
            P(("sensor", "batch"), None),
            P(),
            P(),
            P(),
            P(("sensor", "batch"), None),
            P(),
            P(("sensor", "batch"), None),
            P(),
            P(("sensor", "batch"), None, None),
        ),
        out_specs=(
            P(("sensor", "batch"), None, None),
            P(("sensor", "batch"), None, None),
            P(("sensor", "batch"), None),
            P(),
            P(),
            P(),
            P(),
            P(("sensor", "batch"), None),
            P(),
            P(),
            P(),
            P(("sensor", "batch"), None),
            P(("sensor", "batch"), None),
            P(),
            P(),
            P(),
            P(("sensor", "batch"), None),
            P(),
            P(("sensor", "batch"), None),
            P(),
        ),
        check_vma=False,
    )
```

profile of v0, /device:TPU:0, one launch (start us, length us, event | category | flops | bytes accessed | tf_op | source)
XLA Modules:
  0.0 1364.3 jit_solution(1675318566879572398)
XLA Ops:
  32.4 8.0 gather_fusion.1
  41.0 69.1 %all-gather.6.cloned.1.call-done = bf16[49152,128]{1,0:T(8,128)(2,1)} async-done(((bf16[1536,128]{1,0:T(8,128)(2,1)}), bf16[49152,128]{1,0:T(8,128)(2,1)}) %all-gather.6.cloned.1.call-update) | async-done | bytes 12582928 | tf_op jit(solution)/shard_map/all_gather | solution.py:149
  110.1 14.4 %convolution_convert_fusion = bf16[52,49152]{1,0:T(8,128)(2,1)} fusion(bf16[49152,128]{1,0:T(8,128)(2,1)} %all-gather.6.cloned.1.call-done, f32[52,128]{1,0:T(8,128)S(1)} %convolution_add_fusion.3, f32[52]{0:T(128)S(1)} %reshape.338), kind=kOutput, calls=%fused_computation.4 | convolution fusion | flops 656907264 | bytes 17721552 | tf_op jit(solution)/shard_map/rh,ch->rc/dot_general | solution.py:150
  124.5 8.7 reshape.329
  143.6 27.9 %all-gather.8.cloned.1.call-done = bf16[768,2304]{1,0:T(8,128)(2,1)} async-done(((bf16[24,2304]{1,0:T(8,128)(2,1)}), bf16[768,2304]{1,0:T(8,128)(2,1)}) %all-gather.8.cloned.1.call-update) | async-done | bytes 3538960 | tf_op jit(solution)/shard_map/all_gather | solution.py:155
  182.4 7.3 fusion.73
  189.8 7.8 fusion
  197.6 9.5 fusion.16
  207.1 20.3 %all-gather.10.cloned.1.call-done = bf16[768,768]{1,0:T(8,128)(2,1)} async-done(((bf16[24,768]{1,0:T(8,128)(2,1)}), bf16[768,768]{1,0:T(8,128)(2,1)}) %all-gather.10.cloned.1.call-update) | async-done | bytes 1179664 | tf_op jit(solution)/shard_map/all_gather | solution.py:156
  230.4 62.4 %all-gather.12.cloned.1.call-done = bf16[768,3072]{1,0:T(8,128)(2,1)} async-done(((bf16[24,3072]{1,0:T(8,128)(2,1)}), bf16[768,3072]{1,0:T(8,128)(2,1)}) %all-gather.12.cloned.1.call-update) | async-done | bytes 4718608 | tf_op jit(solution)/shard_map/all_gather | solution.py:157
  292.8 7.1 multiply_convert_fusion.1
  299.9 58.1 %all-gather.14.cloned.1.call-done = bf16[3072,768]{1,0:T(8,128)(2,1)} async-done(((bf16[96,768]{1,0:T(8,128)(2,1)}), bf16[3072,768]{1,0:T(8,128)(2,1)}) %all-gather.14.cloned.1.call-update) | async-done | bytes 4718608 | tf_op jit(solution)/shard_map/all_gather | solution.py:158
  358.0 8.4 convert_reduce_fusion
  377.0 9.4 fusion.17
  386.4 15.0 %multiply_reduce_fusion = (f32[12,516]{1,0:T(8,128)S(1)}, f32[12,516,516]{1,2,0:T(8,128)}) fusion(f32[12,516,516]{1,2,0:T(8,128)} %get-tuple-element.166, f32[12,516]{1,0:T(8,128)S(1)} %log_add_fusion, bf16[516,12,64]{0,2,1:T(8,128)(2,1)} %bitcast.91, bf16[516,12,64]{0,2,1:T(8,128)(2,1)} %bitcast.96), kind=kOutput, calls=%fused_computation.6 | convolution fusion | flops 418548224 | bytes 27195264 | tf_op jit(solution)/shard_map/while/body/eval_jaxpr/qhe,khe->hqk/dot_general | solution.py:84
  401.4 10.0 multiply_convert_fusion
  444.4 10.6 reshape.337
  455.0 10.3 fusion.57
  477.0 8.5 fusion.20
  486.9 8.4 fusion.69
  496.7 8.9 fusion.68
  505.6 12.9 fusion.55
  518.5 25.4 %convolution_add_fusion = f32[49152,128]{1,0:T(8,128)} fusion(f32[49152,128]{1,0:T(8,128)} %fusion.55, f32[52,49152]{1,0:T(8,128)} %reshape.337, f32[52,128]{1,0:T(8,128)S(1)} %copy-done.26, f32[52]{0:T(128)S(1)} %copy-done.33), kind=kOutput, calls=%fused_computation.3 | convolution fusion | flops 670866432 | bytes 60582096 | tf_op jit(solution)/shard_map/rc,rh->ch/dot_general | solution.py:105
  546.8 6.8 multiply_convert_fusion.4
  562.7 72.1 %scatter_fusion = f32[2,1024,832]{2,1,0:T(8,128)} fusion(f32[2,1024,832]{2,1,0:T(8,128)} %broadcast_in_dim.137, s32[512]{0:T(512)S(1)} %bitcast.86, f32[512,832]{1,0:T(8,128)S(1)} %bitcast.94), kind=kCustom, calls=%fused_computation.2 | custom fusion | flops 425984 | bytes 5115904 | tf_op jit(solution)/shard_map/scatter-add | solution.py:260
  634.9 7.9 copy.83
  643.3 41.6 %all-reduce = (f32[768]{0:T(1024)}, f32[8,768]{1,0:T(8,128)}, f32[128]{0:T(128)}, f32[768]{0:T(1024)}, f32[768]{0:T(1024)}, /*index=5*/f32[768]{0:T(1024)}, f32[...) all-reduce(f32[768]{0:T(1024)S(1)} %get-tuple-element.143, ...), channel_id=1, replica_groups=mesh['sensor'=16,'batch'=2] {'sensor','batch'}, use_global_device_ids=true, to_apply=%region_13.14 | all-reduce | flops 15488 | bytes 123904 | tf_op jit(solution)/shard_map/psum | solution.py:274
  685.6 10.0 reduce-scatter.10.cloned.1.call-done
  695.6 125.3 %reduce-scatter.8.cloned.1.call-done = f32[24,2304]{1,0:T(8,128)} async-done(((f32[768,2304]{1,0:T(8,128)}), f32[24,2304]{1,0:T(8,128)}) %reduce-scatter.8.cloned.1.call-update) | async-done | bytes 221200 | tf_op jit(solution)/shard_map/reduce_scatter | solution.py:292
  820.9 141.5 %reduce-scatter.12.cloned.1.call-done = f32[24,3072]{1,0:T(8,128)} async-done(((f32[768,3072]{1,0:T(8,128)}), f32[24,3072]{1,0:T(8,128)}) %reduce-scatter.12.cloned.1.call-update) | async-done | bytes 294928 | tf_op jit(solution)/shard_map/reduce_scatter | solution.py:294
  962.4 142.0 %reduce-scatter.14.cloned.1.call-done = f32[96,768]{1,0:T(8,128)} async-done(((f32[3072,768]{1,0:T(8,128)}), f32[96,768]{1,0:T(8,128)}) %reduce-scatter.14.cloned.1.call-update) | async-done | bytes 294928 | tf_op jit(solution)/shard_map/reduce_scatter | solution.py:295
  1104.3 251.5 %reduce-scatter.6.cloned.1.call-done = f32[1536,128]{1,0:T(8,128)} async-done(((f32[49152,128]{1,0:T(8,128)}), f32[1536,128]{1,0:T(8,128)}) %reduce-scatter.6.cloned.1.call-update) | async-done | bytes 786448 | tf_op jit(solution)/shard_map/reduce_scatter | solution.py:264
  (224 shorter events, 122.0 us)
Async XLA Ops:
  7.2 17.4 %copy-start = (bf16[128,128]{1,0:T(8,128)(2,1)S(1)}, bf16[128,128]{1,0:T(8,128)(2,1)}, u32[]{:S(2)}) copy-start(bf16[128,128]{1,0:T(8,128)(2,1)} %param.34) | copy-start | bytes 98308
  7.2 17.4 %copy-start.45 = (f32[128]{0:T(128)S(1)}, f32[128]{0:T(128)}, u32[]{:S(2)}) copy-start(f32[128]{0:T(128)} %param.35) | copy-start | bytes 1540
  7.2 17.8 %copy-start.20 = (bf16[2,258,768]{2,0,1:T(2,128)(2,1)S(1)}, bf16[2,258,768]{2,0,1:T(2,128)(2,1)}, u32[]{:S(2)}) copy-start(bf16[2,258,768]{2,0,1:T(2,128)(2,1)} %param.49) | copy-start | bytes 2377732
  7.2 102.8 %all-gather.6.cloned.1.call-start = ((), (), s32[]{:S(2)}) async-start(), calls=%async_computation.5 | async-start | bytes 12976128 | tf_op jit(solution)/shard_map/all_gather | solution.py:149
  8.0 163.5 %all-gather.8.cloned.1.call-start = ((), (), s32[]{:S(2)}) async-start(), calls=%async_computation.6 | async-start | bytes 3649536 | tf_op jit(solution)/shard_map/all_gather | solution.py:155
  8.7 218.7 %all-gather.10.cloned.1.call-start = ((), (), s32[]{:S(2)}) async-start(), calls=%async_computation.7 | async-start | bytes 1216512 | tf_op jit(solution)/shard_map/all_gather | solution.py:156
  9.4 283.3 %all-gather.12.cloned.1.call-start = ((), (), s32[]{:S(2)}) async-start(), calls=%async_computation.8 | async-start | bytes 4866048 | tf_op jit(solution)/shard_map/all_gather | solution.py:157
  10.0 348.0 %all-gather.14.cloned.1.call-start = ((), (), s32[]{:S(2)}) async-start(), calls=%async_computation.9 | async-start | bytes 4866048 | tf_op jit(solution)/shard_map/all_gather | solution.py:158
  10.6 674.9 %all-reduce.3.cloned.1.call-start = ((), (), s32[]{:S(2)}) async-start(), calls=%async_computation.10 | async-start | bytes 131072 | tf_op jit(solution)/shard_map/psum | solution.py:274
  24.9 85.2 %copy-start.25 = (f32[52,128]{1,0:T(8,128)}, f32[52,128]{1,0:T(8,128)S(1)}, u32[]{:S(2)}) copy-start(f32[52,128]{1,0:T(8,128)S(1)} %convolution_add_fusion.3) | copy-start | bytes 79876
  25.0 85.1 %copy-start.32 = (f32[52]{0:T(128)}, f32[52]{0:T(128)S(1)}, u32[]{:S(2)}) copy-start(f32[52]{0:T(128)S(1)} %reshape.338) | copy-start | bytes 628
  41.0 95.5 %copy-start.19 = (bf16[2,256,832]{1,2,0:T(8,128)(2,1)}, bf16[2,256,832]{1,2,0:T(8,128)(2,1)S(1)}, u32[]{:S(2)}) copy-start(bf16[2,256,832]{1,2,0:T(8,128)(2,1)S(1)} %copy.65) | copy-start | bytes 2555908
  141.5 30.0 %copy-start.41 = (f32[768]{0:T(1024)S(1)}, f32[768]{0:T(1024)}, u32[]{:S(2)}) copy-start(f32[768]{0:T(1024)} %param.38) | copy-start | bytes 9220
  141.5 30.0 %copy-start.52 = (f32[768]{0:T(1024)S(1)}, f32[768]{0:T(1024)}, u32[]{:S(2)}) copy-start(f32[768]{0:T(1024)} %param.39) | copy-start | bytes 9220
  143.6 32.1 %copy-start.14 = (f32[516,768]{1,0:T(8,128)}, f32[516,768]{1,0:T(8,128)S(1)}, u32[]{:S(2)}) copy-start(f32[516,768]{1,0:T(8,128)S(1)} %reshape.330) | copy-start | bytes 4755460
  182.4 15.2 %copy-start.18 = (bf16[516,768]{0,1:T(8,128)(2,1)}, bf16[516,768]{0,1:T(8,128)(2,1)S(1)}, u32[]{:S(2)}) copy-start(bf16[516,768]{0,1:T(8,128)(2,1)S(1)} %copy.67) | copy-start | bytes 2377732
  197.6 29.8 %copy-start.15 = (f32[516,768]{1,0:T(8,128)S(1)}, f32[516,768]{1,0:T(8,128)}, u32[]{:S(2)}) copy-start(f32[516,768]{1,0:T(8,128)} %copy-done.14) | copy-start | bytes 4755460
  197.6 29.8 %copy-start.51 = (f32[768]{0:T(1024)S(1)}, f32[768]{0:T(1024)}, u32[]{:S(2)}) copy-start(f32[768]{0:T(1024)} %param.42) | copy-start | bytes 9220
  227.4 65.4 %copy-start.42 = (f32[768]{0:T(1024)S(1)}, f32[768]{0:T(1024)}, u32[]{:S(2)}) copy-start(f32[768]{0:T(1024)} %param.43) | copy-start | bytes 9220
  227.4 65.4 %copy-start.49 = (f32[3072]{0:T(1024)S(1)}, f32[3072]{0:T(1024)}, u32[]{:S(2)}) copy-start(f32[3072]{0:T(1024)} %param.46) | copy-start | bytes 36868
  227.4 65.4 %copy-start.54 = (f32[768]{0:T(1024)S(1)}, f32[768]{0:T(1024)}, u32[]{:S(2)}) copy-start(f32[768]{0:T(1024)} %param.44) | copy-start | bytes 9220
  230.0 136.5 %copy-start.11 = (f32[516,768]{1,0:T(8,128)}, f32[516,768]{1,0:T(8,128)S(1)}, u32[]{:S(2)}) copy-start(f32[516,768]{1,0:T(8,128)S(1)} %get-tuple-element.168) | copy-start | bytes 4755460
  230.4 127.7 %copy-start.9 = (f32[516,768]{1,0:T(8,128)S(1)}, f32[516,768]{1,0:T(8,128)}, u32[]{:S(2)}) copy-start(f32[516,768]{1,0:T(8,128)} %reshape.339) | copy-start | bytes 4755460
  377.0 24.4 %slice-start = ((s8[15974400]{0:T(1024)(128)(4,1)}), s8[4194304]{0:T(1024)(128)(4,1)S(1)}, s32[]{:S(2)}) async-start(s8[15974400]{0:T(1024)(128)(4,1)} %bitcast.84), calls=%async_computation.16 | async-start | bytes 8388608
  377.0 24.4 %slice-start.1 = ((s8[15974400]{0:T(1024)(128)(4,1)}), s8[4194304]{0:T(1024)(128)(4,1)S(1)}, s32[]{:S(2)}) async-start(s8[15974400]{0:T(1024)(128)(4,1)} %bitcast.84), calls=%async_computation.17 | async-start | bytes 8388608
  473.1 222.5 %reduce-scatter.10.cloned.1.call-start = ((), (), s32[]{:S(2)}) async-start(), calls=%async_computation.13 | async-start | bytes 2433024 | tf_op jit(solution)/shard_map/reduce_scatter | solution.py:293
  476.9 344.0 %reduce-scatter.8.cloned.1.call-start = ((), (), s32[]{:S(2)}) async-start(), calls=%async_computation.12 | async-start | bytes 7299072 | tf_op jit(solution)/shard_map/reduce_scatter | solution.py:292
  485.5 476.9 %reduce-scatter.12.cloned.1.call-start = ((), (), s32[]{:S(2)}) async-start(), calls=%async_computation.14 | async-start | bytes 9732096 | tf_op jit(solution)/shard_map/reduce_scatter | solution.py:294
  495.3 609.1 %reduce-scatter.14.cloned.1.call-start = ((), (), s32[]{:S(2)}) async-start(), calls=%async_computation.15 | async-start | bytes 9732096 | tf_op jit(solution)/shard_map/reduce_scatter | solution.py:295
  505.5 850.3 %reduce-scatter.6.cloned.1.call-start = ((), (), s32[]{:S(2)}) async-start(), calls=%async_computation.11 | async-start | bytes 25952256 | tf_op jit(solution)/shard_map/reduce_scatter | solution.py:264
  634.8 50.0 %copy-start.34 = (bf16[8,768]{1,0:T(8,128)(2,1)S(1)}, bf16[8,768]{1,0:T(8,128)(2,1)}, u32[]{:S(2)}) copy-start(bf16[8,768]{1,0:T(8,128)(2,1)} %param.33) | copy-start | bytes 36868
  634.9 722.4 %copy-start.1 = (bf16[128,128]{1,0:T(8,128)(2,1)S(1)}, bf16[128,128]{1,0:T(8,128)(2,1)}, u32[]{:S(2)}) copy-start(bf16[128,128]{1,0:T(8,128)(2,1)} %param.34) | copy-start | bytes 98308
  (40 other events, 227.1 us)
Sparse Core Ops, SparseCore 0:
  11.0 99.0 all-gather.5
  113.0 58.4 all-gather.7
  174.4 52.9 all-gather.9
  230.2 62.5 all-gather.11
  295.5 62.4 all-gather.13
  473.2 116.3 all-reduce.2
  595.4 100.1 reduce-scatter.9
  702.8 118.0 reduce-scatter.7
  827.4 134.9 reduce-scatter.11
  969.7 134.5 reduce-scatter.13
  1111.3 244.4 reduce-scatter.5
where the time goes:
time: 1380 us; the launch traced here: 1360 us
  waiting for transfers between devices  911 us (66%)
  matrix products  206 us (15%)
  other arithmetic  112 us (8%)
  local copies, waits for them, and re-layouts  78.3 us (6%)
  blocking collectives  41.6 us (3%)
  between operations  15.1 us (1%)
    reduce_scatter x1, waiting for transfers between devices, local(): lax.psum_scatter(split_dot('rc,rh->ch', grad_kernel, embed_low), ('sensor...  251 us
    reduce_scatter x1, waiting for transfers between devices, local(): lax.psum_scatter(g_down, ('sensor', 'batch'), scatter_dimension=0, tiled=...  142 us
    reduce_scatter x1, waiting for transfers between devices, local(): lax.psum_scatter(g_up, ('sensor', 'batch'), scatter_dimension=0, tiled=True)  141 us
    reduce_scatter x1, waiting for transfers between devices, local(): lax.psum_scatter(g_qkv, ('sensor', 'batch'), scatter_dimension=0, tiled=T...  125 us
    scatter-add x1, other arithmetic, local(): jnp.zeros(pixels.shape, single).at[chip_rows, visible].add(grad_patches)  72.1 us
    all_gather x1, waiting for transfers between devices, local(): generator = lax.all_gather(w_wave2, ('sensor', 'batch'), axis=0, tiled=True)  69.1 us
    all_gather x1, waiting for transfers between devices, local(): lax.all_gather(w_fc1, ('sensor', 'batch'), axis=0, tiled=True)  62.4 us
    all_gather x1, waiting for transfers between devices, local(): lax.all_gather(w_fc2, ('sensor', 'batch'), axis=0, tiled=True)  58.1 us
  transfers between devices with their start and end apart: 11, of which 10 were waited for; matrix products, arithmetic and copies ran while one was open for 20% of the time, Pallas kernels for 0%

commit v1 on v0

v1 whole, which is shorter than its diff:
```python
import functools
import math

import jax
import jax.numpy as jnp
from jax import lax
from jax.experimental import pallas as pl
from jax.experimental.pallas import tpu as pltpu
from jax.sharding import PartitionSpec as P

D = 768
HEADS = 12
HYPER = 128
SIDE = 32
MAXP = 1024
AXES = ("sensor", "batch")

PRECISE = lax.Precision.HIGHEST
EPSILON = 1e-05
MASKED = -1e30
SINGLE = jnp.float32
HALF = jnp.bfloat16


def bit_groups(count):
    bits = count.bit_length() - 1
    high = list(range(3, bits))
    groups = [high[i : i + 2] for i in range(0, len(high), 2)]
    groups.append([b for b in (0, 2) if b < bits])
    if bits > 1:
        groups.append([1])
    return groups


def masks_of(group):
    masks = [0]
    for b in group:
        masks = masks + [m ^ (1 << b) for m in masks]
    return masks


def swap(values, mask, count):
    return lax.ppermute(values, AXES, [(i, i ^ mask) for i in range(count)])


def place_kernel(offsets, splits, index_ref, *refs):
    pieces, refs = refs[: len(offsets)], refs[len(offsets) :]
    outs, refs = refs[: 1 + max(s[0] for s in splits)], refs[1 + max(s[0] for s in splits) :]
    staged, in_sems, out_sems = refs
    me = index_ref[0]
    arrivals, departures = [], []
    first = 0
    for i, piece in enumerate(pieces):
        size = piece.shape[0]
        arrivals.append(
            pltpu.make_async_copy(piece, staged.at[pl.ds(first, size)], in_sems.at[i])
        )
        arrivals[-1].start()
        first += size
    first = 0
    for arrival, masks in zip(arrivals, offsets):
        arrival.wait()
        for t, mask in enumerate(masks):
            for which, slot, start, size in splits:
                target = outs[which].at[me ^ mask]
                departures.append(
                    pltpu.make_async_copy(
                        staged.at[first + t, :, pl.ds(start, size)],
                        target if slot is None else target.at[slot],
                        out_sems.at[len(departures)],
                    )
                )
                departures[-1].start()
        first += len(masks)
    for departure in departures:
        departure.wait()


def place(pieces, masks, splits, shapes, index, count):
    kind = pieces[0].dtype
    row = pieces[0].shape[1:]
    return pl.pallas_call(
        functools.partial(place_kernel, masks, splits),
        out_shape=[jax.ShapeDtypeStruct((count, *s), kind) for s in shapes],
        in_specs=[pl.BlockSpec(memory_space=pltpu.SMEM)]
        + [pl.BlockSpec(memory_space=pl.ANY)] * len(pieces),
        out_specs=[pl.BlockSpec(memory_space=pl.ANY)] * len(shapes),
        scratch_shapes=[
            pltpu.VMEM((count, *row), kind),
            pltpu.SemaphoreType.DMA((len(pieces),)),
            pltpu.SemaphoreType.DMA((count * len(splits),)),
        ],
        compiler_params=pltpu.CompilerParams(vmem_limit_bytes=32 * 2**20),
        cost_estimate=pl.CostEstimate(
            flops=0,
            bytes_accessed=4 * count * math.prod(row),
            transcendentals=0,
        ),
        name="place",
    )(index, *pieces)


def gather(shards, index, count):
    rows = min(s.shape[0] for s in shards)
    columns, splits, shapes = [], [], []
    start = 0
    for which, shard in enumerate(shards):
        parts = shard.shape[0] // rows
        shapes.append((parts, rows, shard.shape[1]) if parts > 1 else (rows, shard.shape[1]))
        for i in range(parts):
            columns.append(shard[i * rows : (i + 1) * rows])
            splits.append((which, i if parts > 1 else None, start, shard.shape[1]))
            start += shard.shape[1]
    groups = bit_groups(count)
    data, masks = jnp.concatenate(columns, axis=1)[None], [0]
    for group in groups[:-2]:
        ours = masks_of(group)
        data = jnp.concatenate(
            [data] + [swap(data, m, count) for m in ours[1:]], axis=0
        )
        masks = [m ^ q for m in ours for q in masks]
    pieces = [(masks, data)]
    for group in groups[-2:]:
        pieces = pieces + [
            ([m ^ q for q in held], swap(piece, m, count))
            for m in masks_of(group)[1:]
            for held, piece in pieces
        ]
    wholes = place(
        [p for _, p in pieces], [m for m, _ in pieces], splits, shapes, index, count
    )
    return [w.reshape(-1, w.shape[-1]) for w in wholes]


def chosen_half(values, bits, group, mask, index):
    starts, sizes, shape = [], [], []
    for b in bits:
        if b in group:
            starts.append(((index[0] ^ mask) >> b) & 1)
            sizes.append(1)
        else:
            starts.append(0)
            sizes.append(2)
            shape.append(2)
    tail = values.shape[len(bits) :]
    zeros = [0] * len(tail)
    return lax.dynamic_slice(values, starts + zeros, sizes + list(tail)).reshape(
        *shape, *tail
    )


def scatter(wholes, index, count):
    bits = list(range(count.bit_length() - 2, -1, -1))
    rows = min(w.shape[0] for w in wholes) // count
    kind = wholes[0].dtype
    views, columns, start = [], [], 0
    for whole in wholes:
        k = whole.shape[0] // count // rows
        view = whole.reshape([2] * len(bits) + [k, rows, whole.shape[1]])
        for i in range(k):
            columns.append((len(views), i, start, whole.shape[1]))
            start += whole.shape[1]
        views.append(view)
    received = []
    done = []

    def part(mask):
        pieces = []
        own = [chosen_half(v, bits, done, mask, index) for v in views]
        others = [chosen_half(v, left, done, mask, index) for v, left in received]
        for which, i, first, width in columns:
            piece = own[which][..., i, :, :]
            if others:
                piece = piece.astype(SINGLE)
                for other in others:
                    piece = piece + other[..., first : first + width].astype(SINGLE)
            pieces.append(piece)
        return pieces

    for group in reversed(bit_groups(count)):
        done = done + group
        arrived = []
        for m in masks_of(group)[1:]:
            sent = jnp.concatenate([p.astype(kind) for p in part(m)], axis=-1)
            arrived.append((swap(sent, m, count), [b for b in bits if b not in done]))
        received = received + arrived
    pieces = part(0)
    out = []
    for which in range(len(views)):
        mine = [p for p, c in zip(pieces, columns) if c[0] == which]
        out.append(jnp.concatenate(mine, axis=0) if len(mine) > 1 else mine[0])
    return out


def tree_sum(values):
    while len(values) > 1:
        values = [values[i] + values[i + 1] for i in range(0, len(values), 2)]
    return values[0]


def total_over(values, count):
    for group in reversed(bit_groups(count)):
        values = tree_sum(
            [values if m == 0 else swap(values, m, count) for m in masks_of(group)]
        )
    return values


def scores_of(keyed, query, lanes, key_ok):
    own = jnp.where(lanes, keyed, jnp.zeros_like(keyed))
    scores = lax.dot_general(
        own, query, (((1,), (1,)), ((), ())), preferred_element_type=SINGLE
    )
    scores = jnp.where(key_ok, scores, MASKED)
    expd = jnp.exp(scores - jnp.max(scores, axis=0, keepdims=True))
    return expd / jnp.sum(expd, axis=0, keepdims=True)


def over_rows(left, right):
    return lax.dot_general(
        left, right, (((0,), (0,)), ((), ())), preferred_element_type=SINGLE
    )


def attend_kernel(width, scale, count_ref, qkv_ref, out_ref):
    rows = qkv_ref.shape[1]
    head_dim = width // HEADS
    limit = count_ref[pl.program_id(0)]
    lane = lax.broadcasted_iota(jnp.int32, (rows, 128), 1) // head_dim
    key_ok = lax.broadcasted_iota(jnp.int32, (rows, rows), 0) < limit

    @pl.loop(0, width // 128)
    def _(pair):
        start = pl.multiple_of(pair * 128, 128)
        query = qkv_ref[0, :, pl.ds(start, 128)] * jnp.asarray(scale, HALF)
        keyed = qkv_ref[0, :, pl.ds(pl.multiple_of(width + start, 128), 128)]
        valued = qkv_ref[0, :, pl.ds(pl.multiple_of(2 * width + start, 128), 128)]
        result = jnp.zeros((rows, 128), SINGLE)
        for head in range(128 // head_dim):
            probs = scores_of(keyed, query, lane == head, key_ok)
            result = jnp.where(
                lane == head, over_rows(probs.astype(HALF), valued), result
            )
        out_ref[0, :, pl.ds(start, 128)] = result.astype(HALF)


def attend_back_kernel(width, scale, count_ref, qkv_ref, up_ref, out_ref):
    rows = qkv_ref.shape[1]
    head_dim = width // HEADS
    limit = count_ref[pl.program_id(0)]
    lane = lax.broadcasted_iota(jnp.int32, (rows, 128), 1) // head_dim
    key_ok = lax.broadcasted_iota(jnp.int32, (rows, rows), 0) < limit

    @pl.loop(0, width // 128)
    def _(pair):
        start = pl.multiple_of(pair * 128, 128)
        at_key = pl.multiple_of(width + start, 128)
        at_value = pl.multiple_of(2 * width + start, 128)
        query = qkv_ref[0, :, pl.ds(start, 128)] * jnp.asarray(scale, HALF)
        keyed = qkv_ref[0, :, pl.ds(at_key, 128)]
        valued = qkv_ref[0, :, pl.ds(at_value, 128)]
        upstream = up_ref[0, :, pl.ds(start, 128)]
        grad_q = jnp.zeros((rows, 128), SINGLE)
        grad_k = jnp.zeros((rows, 128), SINGLE)
        grad_v = jnp.zeros((rows, 128), SINGLE)
        for head in range(128 // head_dim):
            own = lane == head
            probs = scores_of(keyed, query, own, key_ok)
            grad_v = jnp.where(
                own,
                jnp.dot(probs.astype(HALF), upstream, preferred_element_type=SINGLE),
                grad_v,
            )
            grad_prob = lax.dot_general(
                jnp.where(own, valued, jnp.zeros_like(valued)),
                upstream,
                (((1,), (1,)), ((), ())),
                preferred_element_type=SINGLE,
            )
            inner = jnp.sum(probs * grad_prob, axis=0, keepdims=True)
            grad_score = (probs * (grad_prob - inner)).astype(HALF)
            grad_k = jnp.where(
                own, jnp.dot(grad_score, query, preferred_element_type=SINGLE), grad_k
            )
            grad_q = jnp.where(own, over_rows(grad_score, keyed), grad_q)
        out_ref[0, :, pl.ds(start, 128)] = (grad_q * scale).astype(HALF)
        out_ref[0, :, pl.ds(at_key, 128)] = grad_k.astype(HALF)
        out_ref[0, :, pl.ds(at_value, 128)] = grad_v.astype(HALF)


def attention_call(kernel, name, counts, arrays, out_width, flops):
    chips, rows = arrays[0].shape[:2]

    def spec(columns):
        return pl.BlockSpec((1, rows, columns), lambda c, counts: (c, 0, 0))

    return pl.pallas_call(
        kernel,
        out_shape=jax.ShapeDtypeStruct((chips, rows, out_width), HALF),
        grid_spec=pltpu.PrefetchScalarGridSpec(
            num_scalar_prefetch=1,
            grid=(chips,),
            in_specs=[spec(a.shape[2]) for a in arrays],
            out_specs=spec(out_width),
        ),
        compiler_params=pltpu.CompilerParams(vmem_limit_bytes=40 * 2**20),
        cost_estimate=pl.CostEstimate(
            flops=flops, bytes_accessed=10 * 2**20, transcendentals=2 * 2**20
        ),
        name=name,
    )(counts, *arrays)


def wave_code(wavelengths):
    halfwidth = HYPER // 2
    freqs = 10000.0 ** (-jnp.arange(halfwidth, dtype=SINGLE) / halfwidth)
    angles = (wavelengths * 1000.0)[:, :, None] * freqs
    return jnp.concatenate([jnp.sin(angles), jnp.cos(angles)], axis=-1)


def norm_forward(values, gain, offset):
    center = values - jnp.mean(values, axis=-1, keepdims=True)
    inv_std = lax.rsqrt(jnp.mean(center * center, axis=-1, keepdims=True) + EPSILON)
    normed = center * inv_std
    return (normed * gain + offset, normed, inv_std)


def norm_backward(upstream, normed, inv_std, gain):
    scaled = upstream * gain
    back = inv_std * (
        scaled
        - jnp.mean(scaled, axis=-1, keepdims=True)
        - normed * jnp.mean(scaled * normed, axis=-1, keepdims=True)
    )
    return (back, jnp.sum(upstream * normed, axis=0), jnp.sum(upstream, axis=0))


def gelu_parts(values):
    cumul = 0.5 * (1.0 + lax.erf(values * 0.5**0.5))
    density = jnp.exp(-0.5 * values * values) * (2.0 * math.pi) ** (-0.5)
    return (values * cumul, cumul + values * density)


def split_dot(form, exact, other):
    upper = exact.astype(HALF)
    lower = (exact - upper.astype(SINGLE)).astype(HALF)
    first_term = jnp.einsum(form, upper, other, preferred_element_type=SINGLE)
    return first_term + jnp.einsum(form, lower, other, preferred_element_type=SINGLE)


def local(
    count,
    pixels,
    visible,
    chip_size,
    sensor_id,
    band_count,
    wavelengths,
    time_place,
    cls_token,
    w_meta,
    w_wave1,
    wave1_bias,
    w_wave2,
    patch_bias,
    ln1_gain,
    ln1_bias,
    w_qkv,
    w_out,
    out_bias,
    ln2_gain,
    ln2_bias,
    w_fc1,
    fc1_bias,
    w_fc2,
    fc2_bias,
    cotangent,
):
    chips, patches_all, pix_width = pixels.shape
    sensors, bands = wavelengths.shape
    length, width = cotangent.shape[1:]
    seen = visible.shape[1]
    lead = length - seen
    rows = -(-length // 16) * 16
    rows_all = chips * rows
    spots = pix_width // bands
    scale = (width // HEADS) ** (-0.5)
    me = lax.axis_index(AXES).astype(jnp.int32).reshape(1)

    code = wave_code(wavelengths).reshape(sensors * bands, -1)
    band_mask = (
        (jnp.arange(bands)[None, :] < band_count[:, None]).astype(SINGLE).reshape(-1, 1)
    )
    pre_act = jnp.dot(code, w_wave1.astype(SINGLE), precision=PRECISE) + wave1_bias
    activ, activ_slope = gelu_parts(pre_act)
    embed_low = (activ * band_mask).astype(HALF)
    columns = w_wave2.shape[0]
    held = max(1, columns // width)
    per_row = columns // held
    pieces = width // per_row
    wave2_own = w_wave2.reshape(held, per_row, -1)
    kernel_own = (
        jnp.einsum("rh,pch->prc", embed_low, wave2_own, preferred_element_type=SINGLE)
        .astype(HALF)
        .reshape(held * sensors * bands, per_row)
    )
    generated = gather([kernel_own], me, count)[0]
    generated = (
        generated.reshape(spots // held, pieces, held * sensors * bands, per_row)
        if pieces > 1
        else generated
    )
    if pieces > 1:
        generated = generated.transpose(0, 2, 1, 3)
    generated = generated.reshape(spots * sensors * bands, width)

    proj_qkv, proj_out = gather([w_qkv, w_out], me, count)
    proj_down, proj_up = gather([w_fc2, w_fc1], me, count)

    spot_of = jnp.pad(visible, ((0, 0), (lead, rows - length)), constant_values=-1)
    token = jnp.arange(rows)
    is_patch = ((token >= lead) & (token < length)).astype(SINGLE)[None, :, None]
    chosen = (spot_of[:, :, None] == jnp.arange(patches_all)[None, None, :]).astype(HALF)
    patches = jnp.einsum(
        "ctp,cpv->ctv", chosen, pixels, preferred_element_type=SINGLE
    ).astype(HALF)
    row_ids = jnp.arange(spots * sensors * bands)
    row_spot, row_sensor, row_band = (
        row_ids // (sensors * bands),
        (row_ids // bands) % sensors,
        row_ids % bands,
    )
    source = jnp.where(
        row_sensor[None, :] == sensor_id[:, None], (row_band * spots + row_spot)[None, :], -1
    )
    spread = (jnp.arange(pix_width)[None, :, None] == source[:, None, :]).astype(HALF)
    patches_wide = (
        jnp.einsum("ctv,cvr->ctr", patches, spread, preferred_element_type=SINGLE)
        .astype(HALF)
        .reshape(rows_all, -1)
    )
    kern_chip = jnp.einsum(
        "cvr,rd->cvd", spread, generated, preferred_element_type=SINGLE
    ).astype(HALF)

    side_len = jnp.where(chip_size == MAXP, SIDE, SIDE // 2).astype(jnp.int32)[:, None]
    quarter = width // 4
    freqs = 10000.0 ** (-jnp.arange(quarter, dtype=SINGLE) / quarter)
    angles = jnp.arange(SIDE, dtype=SINGLE)[:, None] * freqs
    table = jnp.concatenate([jnp.sin(angles), jnp.cos(angles)], axis=-1)

    def places(steps):
        steps = jnp.where(spot_of < 0, -1, steps)
        hot = (steps[:, :, None] == jnp.arange(SIDE)).astype(SINGLE)
        return jnp.einsum("cts,se->cte", hot, table, precision=PRECISE)

    base = jnp.concatenate(
        [places(spot_of // side_len), places(spot_of % side_len)], axis=-1
    )
    base = base + patch_bias * is_patch
    meta_tok = jnp.dot(time_place, w_meta.astype(SINGLE), precision=PRECISE)
    base = jnp.where((token == 0)[None, :, None], cls_token[None, None, :], base)
    base = jnp.where((token == 1)[None, :, None], meta_tok[:, None, :], base)
    base = base.reshape(rows_all, width)

    counts = (lead + chip_size // 4).astype(jnp.int32)
    keep_rows = (
        (token[None, :] < counts[:, None]).reshape(rows_all, 1).astype(SINGLE)
    )
    grad_final = (
        jnp.pad(cotangent, ((0, 0), (0, rows - length), (0, 0)))
        .reshape(rows_all, width)
        .astype(SINGLE)
        * keep_rows
    )
    grad_branch = grad_final.astype(HALF)
    g_fc2_bias = jnp.sum(grad_final, axis=0)

    start = (
        jnp.dot(patches_wide, generated, preferred_element_type=SINGLE) + base
    )
    normed_one, hat_one, inv_one = norm_forward(start, ln1_gain, ln1_bias)
    normed_one = normed_one.astype(HALF)
    joined = jnp.dot(normed_one, proj_qkv, preferred_element_type=SINGLE).astype(HALF)
    joined = joined.reshape(chips, rows, -1)
    attn = attention_call(
        functools.partial(attend_kernel, width, scale),
        "attend",
        counts,
        (joined,),
        width,
        4 * chips * rows * rows * width,
    ).reshape(rows_all, width)
    middle = start + jnp.dot(attn, proj_out, preferred_element_type=SINGLE) + out_bias
    normed_two, hat_two, inv_two = norm_forward(middle, ln2_gain, ln2_bias)
    normed_two = normed_two.astype(HALF)
    grad_hidden = jnp.einsum(
        "rd,fd->rf", grad_branch, proj_down, preferred_element_type=SINGLE
    )
    pre_up = jnp.dot(normed_two, proj_up, preferred_element_type=SINGLE) + fc1_bias
    hidden_f, hidden_slope = gelu_parts(pre_up)
    hidden = hidden_f.astype(HALF)
    grad_up = (grad_hidden * hidden_slope).astype(HALF)

    g_down = jnp.einsum("rf,rd->fd", hidden, grad_branch, preferred_element_type=SINGLE)
    g_up = jnp.einsum("rd,rf->df", normed_two, grad_up, preferred_element_type=SINGLE)
    g_down, g_up = scatter([g_down.astype(HALF), g_up.astype(HALF)], me, count)
    g_fc1_bias = jnp.sum(grad_up.astype(SINGLE), axis=0)
    grad_norm_two = jnp.einsum(
        "rf,df->rd", grad_up, proj_up, preferred_element_type=SINGLE
    )
    back_two, g_ln2_gain, g_ln2_bias = norm_backward(
        grad_norm_two, hat_two, inv_two, ln2_gain
    )
    grad_middle = grad_final + back_two
    grad_attn_out = grad_middle.astype(HALF)
    g_out_bias = jnp.sum(grad_attn_out.astype(SINGLE), axis=0)
    g_out = jnp.einsum("rd,re->de", attn, grad_attn_out, preferred_element_type=SINGLE)
    grad_attn = (
        jnp.einsum("re,de->rd", grad_attn_out, proj_out, preferred_element_type=SINGLE)
        .astype(HALF)
        .reshape(chips, rows, width)
    )
    grad_joined = attention_call(
        functools.partial(attend_back_kernel, width, scale),
        "attend_back",
        counts,
        (joined, grad_attn),
        3 * width,
        10 * chips * rows * rows * width,
    ).reshape(rows_all, -1)
    g_qkv = jnp.einsum(
        "rd,re->de", normed_one, grad_joined, preferred_element_type=SINGLE
    )
    g_qkv, g_out = scatter([g_qkv.astype(HALF), g_out.astype(HALF)], me, count)
    grad_norm_one = jnp.einsum(
        "re,de->rd", grad_joined, proj_qkv, preferred_element_type=SINGLE
    )
    back_one, g_ln1_gain, g_ln1_bias = norm_backward(
        grad_norm_one, hat_one, inv_one, ln1_gain
    )
    grad_start = grad_middle + back_one
    grad_embedded = (
        (grad_start.reshape(chips, rows, width) * is_patch)
        .astype(HALF)
        .reshape(rows_all, width)
    )
    kern_terms = jnp.einsum(
        "rk,rd->kd", patches_wide, grad_embedded, preferred_element_type=SINGLE
    ).astype(HALF)
    if pieces > 1:
        kern_terms = kern_terms.reshape(
            spots // held, held * sensors * bands, pieces, per_row
        ).transpose(0, 2, 1, 3)
    grad_kernel = scatter([kern_terms.reshape(-1, per_row)], me, count)[0]
    grad_kernel = grad_kernel.reshape(held, sensors * bands, per_row)
    grad_embed = split_dot("prc,pch->rh", grad_kernel, wave2_own)
    g_wave2 = split_dot("prc,rh->pch", grad_kernel, embed_low).reshape(columns, -1)
    by_chip = grad_start.reshape(chips, rows, width)
    g_cls = jnp.sum(by_chip[:, 0, :], axis=0)
    grad_meta = by_chip[:, 1, :]
    g_w_meta = jnp.einsum("cm,cd->md", time_place, grad_meta, precision=PRECISE)
    g_time_place = jnp.einsum(
        "cd,md->cm", grad_meta, w_meta.astype(SINGLE), precision=PRECISE
    )
    g_patch_bias = jnp.sum(by_chip * is_patch, axis=(0, 1))
    meta_rows = time_place.shape[1]
    small = total_over(
        jnp.concatenate(
            [
                g_w_meta,
                g_fc1_bias.reshape(-1, width),
                g_cls[None],
                g_patch_bias[None],
                g_ln1_gain[None],
                g_ln1_bias[None],
                g_out_bias[None],
                g_ln2_gain[None],
                g_ln2_bias[None],
                g_fc2_bias[None],
                jnp.pad(grad_embed.reshape(-1), (0, -grad_embed.size % width)).reshape(
                    -1, width
                ),
            ],
            axis=0,
        ),
        count,
    )
    base_row = meta_rows + fc1_bias.shape[0] // width
    grad_embed = small[base_row + 8 :].reshape(-1)[: grad_embed.size]
    grad_embed = grad_embed.reshape(sensors * bands, -1)
    grad_pre = grad_embed * band_mask * activ_slope
    g_wave1 = jnp.einsum("rh,rk->hk", code, grad_pre, precision=PRECISE)
    g_wave1_bias = jnp.sum(grad_pre, axis=0)


    scattered = jnp.einsum(
        "ctp,ctd->cpd",
        chosen,
        grad_embedded.reshape(chips, rows, width),
        preferred_element_type=SINGLE,
    ).astype(HALF)
    g_pixels = jnp.einsum(
        "cpd,cvd->cpv", scattered, kern_chip, preferred_element_type=SINGLE
    )
    final = middle + jnp.dot(hidden, proj_down, preferred_element_type=SINGLE) + fc2_bias
    mixed = (final * keep_rows).astype(HALF).reshape(chips, rows, width)[:, :length]
    return (
        mixed,
        g_pixels,
        g_time_place,
        small[base_row],
        small[:meta_rows],
        g_wave1,
        g_wave1_bias,
        g_wave2,
        small[base_row + 1],
        small[base_row + 2],
        small[base_row + 3],
        g_qkv,
        g_out,
        small[base_row + 4],
        small[base_row + 5],
        small[base_row + 6],
        g_up,
        small[meta_rows:base_row].reshape(-1),
        g_down,
        small[base_row + 7],
    )


def solution(mesh):
    count = math.prod(mesh.shape[a] for a in AXES)
    split = lambda rank: P(AXES, *([None] * (rank - 1)))
    return jax.shard_map(
        functools.partial(local, count),
        mesh=mesh,
        in_specs=(
            split(3),
            split(2),
            split(1),
            split(1),
            P(),
            P(),
            split(2),
            P(),
            P(),
            P(),
            P(),
            split(2),
            P(),
            P(),
            P(),
            split(2),
            split(2),
            P(),
            P(),
            P(),
            split(2),
            P(),
            split(2),
            P(),
            split(3),
        ),
        out_specs=(
            split(3),
            split(3),
            split(2),
            P(),
            P(),
            P(),
            P(),
            split(2),
            P(),
            P(),
            P(),
            split(2),
            split(2),
            P(),
            P(),
            P(),
            split(2),
            P(),
            split(2),
            P(),
        ),
        check_vma=False,
    )
```

time: 1380 us -> 492 us (0.36)
  waiting for transfers between devices: 911 us -> 167 us
  matrix products: 206 us -> 95.2 us
  starting transfers between devices: 0.44 us -> 61.8 us
  other arithmetic: 112 us -> 59.7 us
  Pallas kernels: 0 us -> 49.4 us
  blocking collectives: 41.6 us -> 0 us
  local copies, waits for them, and re-layouts: 78.3 us -> 49.4 us
    reduce_scatter x5 -> x0, waiting for transfers between devices: 670 us -> none  [the longest x1 251 us: local(): lax.psum_scatter(split_dot('rc,rh->ch', grad_kernel, embed_low), ('sensor...]
    all_gather x5 -> x0, waiting for transfers between devices: 238 us -> none  [the longest x1 69.1 us: local(): generator = lax.all_gather(w_wave2, ('sensor', 'batch'), axis=0, tiled=True)]
    ppermute x0 -> x58, waiting for transfers between devices: none -> 167 us  [swap(): return lax.ppermute(values, AXES, [(i, i ^ mask) for i in range(count)])]
    dot_general x31 -> x27, matrix products: 204 us -> 94 us  [the longest x1 11.4 us: local(): jnp.einsum('cvr,rd->cvd', spread, generated, preferred_element_type=SINGLE)]
    scatter-add x1 -> x0, other arithmetic: 72.1 us -> none  [local(): jnp.zeros(pixels.shape, single).at[chip_rows, visible].add(grad_patches)]
    ppermute x0 -> x58, starting transfers between devices: none -> 61.8 us  [swap(): return lax.ppermute(values, AXES, [(i, i ^ mask) for i in range(count)])]
    pallas_call x0 -> x5, Pallas kernels: none -> 49.4 us  [the longest x2 30.1 us: attention_call(): pl.pallas_call(kernel, out_shape=jax.ShapeDtypeStruct((chips, rows, out_w...]
    psum x1 -> x0, blocking collectives: 41.6 us -> none  [local(): lax.psum((g_cls, g_w_meta, g_wave1, g_wave1_bias, g_patch_bias, g_ln1_gai...]
  transfers between devices with their start and end apart: 11 -> 58, of which waited for: 10 -> 22; matrix products, arithmetic and copies ran while one was open for 20% -> 26% of each run, Pallas kernels for 0% -> 5%
where the time goes in v1:
time: 492 us; the launch traced here: 486 us
  waiting for transfers between devices  167 us (34%)
  matrix products  95.2 us (19%)
  starting transfers between devices  61.8 us (13%)
  other arithmetic  59.7 us (12%)
  local copies, waits for them, and re-layouts  49.4 us (10%)
  Pallas kernels  49.4 us (10%)
    ppermute x58, waiting for transfers between devices, swap(): return lax.ppermute(values, AXES, [(i, i ^ mask) for i in range(count)])  167 us
    ppermute x58, starting transfers between devices, swap(): return lax.ppermute(values, AXES, [(i, i ^ mask) for i in range(count)])  61.8 us
    pallas_call x2, Pallas kernels, attention_call(): pl.pallas_call(kernel, out_shape=jax.ShapeDtypeStruct((chips, rows, out_w...  30.1 us
    unnamed x191, local copies, waits for them, and re-layouts  28.2 us
    pallas_call x3, Pallas kernels, place(): pl.pallas_call(functools.partial(place_kernel, masks, splits), out_shape=...  19.3 us
    unnamed x26, other arithmetic  14.8 us
    dot_general x1, matrix products, local(): jnp.einsum('cvr,rd->cvd', spread, generated, preferred_element_type=SINGLE)  11.4 us
  transfers between devices with their start and end apart: 58, of which 22 were waited for; matrix products, arithmetic and copies ran while one was open for 26% of the time, Pallas kernels for 5%

profile of v1, /device:TPU:0, one launch (start us, length us, event | category | flops | bytes accessed | tf_op | source)
XLA Modules:
  0.0 485.7 jit_solution(4200440106289739193)
XLA Ops:
  2.4 5.0 %collective-permute-start.12 = (bf16[1,24,3072]{2,1,0:T(8,128)(2,1)}, bf16[1,24,3072]{2,1,0:T(8,128)(2,1)}, u32[]{:S(2)}, u32[]{:S(2)}) collective-permute-start(bf16[1,24,3072]{2,1,0:T(8,128)(2,1)} %maximum_bitcast_fusion), channel_id=1, source_target_pairs={{0,24},{1,25},{2,26},{3,27},{4,28},{5,29},{6,30},{7,31},{8,16},{9,... | collective-permute-start | bytes 442376 | tf_op jit(solution)/shard_map/ppermute | solution.py:43
  16.3 3.8 collective-permute-start.2
  45.9 7.2 %collective-permute-done.22 = bf16[1,24,6144]{2,1,0:T(8,128)(2,1)S(1)} collective-permute-done((bf16[1,24,6144]{2,1,0:T(8,128)(2,1)}, bf16[1,24,6144]{2,1,0:T(8,128)(2,1)S(1)}, u32[]{:S(2)}, u32[]{:S(2)}) %collective-permute-start.22) | collective-permute-done | bytes 294944 | tf_op jit(solution)/shard_map/ppermute | solution.py:43
  56.9 8.2 %collective-permute-done.21 = bf16[1,24,6144]{2,1,0:T(8,128)(2,1)S(1)} collective-permute-done((bf16[1,24,6144]{2,1,0:T(8,128)(2,1)}, bf16[1,24,6144]{2,1,0:T(8,128)(2,1)S(1)}, u32[]{:S(2)}, u32[]{:S(2)}) %collective-permute-start.21) | collective-permute-done | bytes 294944 | tf_op jit(solution)/shard_map/ppermute | solution.py:43
  76.8 7.5 %fusion.10 = bf16[2,272,3328]{2,1,0:T(8,128)(2,1)} fusion(s32[2,3328]{1,0:T(2,128)S(1)} %compare_select_fusion, bf16[2,1024,832]{1,2,0:T(8,128)(2,1)S(1)} %copy-done, s32[2,272]{1,0:T(2,128)S(1)} %get-tuple-element.116), kind=kOutput, calls=%fused_computation.16 | convolution fusion | flops 3947857920 | bytes 7057536 | tf_op jit(solution)/shard_map/ctv,cvr->ctr/dot_general | solution.py:438
  84.2 6.2 %collective-permute-done.5.refs_3_ = bf16[4,104,768]{2,1,0:T(8,128)(2,1)} collective-permute-done((bf16[4,104,768]{2,1,0:T(8,128)(2,1)}, bf16[4,104,768]{2,1,0:T(8,128)(2,1)}, u32[]{:S(2)}, u32[]{:S(2)}) %collective-permute-start.5) | collective-permute-done | bytes 639008 | tf_op jit(solution)/shard_map/ppermute | solution.py:43
  90.4 9.5 %collective-permute-done.4.refs_2_ = bf16[4,104,768]{2,1,0:T(8,128)(2,1)} collective-permute-done((bf16[4,104,768]{2,1,0:T(8,128)(2,1)}, bf16[4,104,768]{2,1,0:T(8,128)(2,1)}, u32[]{:S(2)}, u32[]{:S(2)}) %collective-permute-start.4) | collective-permute-done | bytes 639008 | tf_op jit(solution)/shard_map/ppermute | solution.py:43
  112.7 8.2 %place.3 = bf16[32,104,768]{2,1,0:T(8,128)(2,1)S(1)} custom-call(s32[1]{0:T(128)} %bitcast.1.index_ref, bf16[4,104,768]{2,1,0:T(8,128)(2,1)} %constant_dynamic-update-slice_fusion.refs_0_, bf16[4,104,768]{2,1,0:T(8,128)(2,1)} %collective-permute-done.3.refs_1_, bf16[4,104,768]{2,1,0:T(8,128)(2,1)} %collective-permute-done.4.refs_2_, ...), custom_call_target="tpu_custom_call" | custom-call | bytes 10223616 | tf_op jit(solution)/shard_map/place/pallas_call | solution.py:82
  123.3 4.3 fusion.18
  131.2 4.3 convolution_convert_fusion.3
  135.5 12.8 %attend.1 = bf16[2,272,768]{2,1,0:T(8,128)(2,1)S(1)} custom-call(s32[2]{0:T(128)S(1)} %get-tuple-element.123.count_ref, bf16[2,272,2304]{2,1,0:T(8,128)(2,1)S(1)} %bitcast.561), custom_call_target="tpu_custom_call" | custom-call | flops 454557696 | bytes 10485760 | tf_op jit(solution)/shard_map/attend/pallas_call | solution.py:297
  149.8 13.6 %collective-permute-done.24.refs_2_ = bf16[4,24,6144]{2,1,0:T(8,128)(2,1)} collective-permute-done((bf16[4,24,6144]{2,1,0:T(8,128)(2,1)S(1)}, bf16[4,24,6144]{2,1,0:T(8,128)(2,1)}, u32[]{:S(2)}, u32[]{:S(2)}) %collective-permute-start.24) | collective-permute-done | bytes 1179680 | tf_op jit(solution)/shard_map/ppermute | solution.py:43
  163.9 11.4 %fusion = bf16[2,832,768]{2,1,0:T(8,128)(2,1)} fusion(bf16[3328,768,1]{1,0,2:T(8,128)(2,1)S(1)} %bitcast.560, s32[2,3328]{1,0:T(2,128)S(1)} %copy-done.49), kind=kOutput, calls=%fused_computation.1 | convolution fusion | flops 8511586304 | bytes 7694336 | tf_op jit(solution)/shard_map/cvr,rd->cvd/dot_general | solution.py:442
  175.3 7.4 %place.5 = (bf16[32,4,24,768]{3,2,1,0:T(8,128)(2,1)S(1)}, bf16[32,24,3072]{2,1,0:T(8,128)(2,1)S(1)}) custom-call(s32[1]{0:T(128)} %bitcast.1.index_ref, bf16[4,24,6144]{2,1,0:T(8,128)(2,1)S(1)} %pad_maximum_fusion.1.refs_0_, bf16[4,24,6144]{2,1,0:T(8,128)(2,1)} %collective-permute-done.23.refs_1_, bf16[4,24,6144]{2,1,0:T(8,128)(2,1)} %collective-permute-done.24.refs_2_, ...), custom_call_target="tpu_custom_call" | custom-call | bytes 18874368 | tf_op jit(solution)/shard_map/place/pallas_call | solution.py:82
  182.7 6.8 %multiply_convert_fusion = (bf16[544,3072]{1,0:T(8,128)(2,1)}, f32[544,3072]{1,0:T(8,128)}) fusion(f32[3072]{0:T(1024)S(1)} %copy-done.74, bf16[768,3072]{1,0:T(8,128)(2,1)S(1)} %bitcast.568, f32[544,768]{1,0:T(8,128)S(1)} %get-tuple-element.128, f32[768]{0:T(1024)S(1)} %copy-done.78, f32[768]{0:T(1024)S(1)} %copy-done.64, f32[544]{0:T(1024)S(1)} %add_rsqrt_fusion, ...), kind=kOutput, calls=%fused_computation.14 | convolution fusion | flops 2579030016 | bytes 16439552 | tf_op jit(solution)/shard_map/dot_general | solution.py:500
  189.5 6.6 %convert_reduce_fusion = (f32[3072]{0:T(1024)S(1)}, bf16[544,3072]{1,0:T(8,128)(2,1)S(1)}) fusion(f32[544,3072]{1,0:T(8,128)} %get-tuple-element.130, f32[3072]{0:T(1024)S(1)} %copy-done.74, bf16[544,768]{1,0:T(8,128)(2,1)S(1)} %bitcast.627, bf16[3072,768]{1,0:T(8,128)(2,1)S(1)} %bitcast.566), kind=kOutput, calls=%fused_computation.13 | convolution fusion | flops 2588636160 | bytes 15605760 | tf_op jit(solution)/shard_map/rd,fd->rf/dot_general | solution.py:497
  204.4 17.3 %attend_back.1 = bf16[2,272,2304]{2,1,0:T(8,128)(2,1)S(1)} custom-call(s32[2]{0:T(128)S(1)} %get-tuple-element.123.count_ref, bf16[2,272,2304]{2,1,0:T(8,128)(2,1)S(1)} %bitcast.562, bf16[2,272,768]{2,1,0:T(8,128)(2,1)S(1)} %bitcast.565), custom_call_target="tpu_custom_call" | custom-call | flops 1136394240 | bytes 10485760 | tf_op jit(solution)/shard_map/attend_back/pallas_call | solution.py:297
  224.3 4.7 convolution_convert_fusion
  231.6 6.3 %bitcast_convert_fusion = bf16[3328,768]{1,0:T(8,128)(2,1)} fusion(bf16[2,272,3328]{2,1,0:T(8,128)(2,1)S(1)} %copy-done.20, f32[2,272,768]{2,1,0:T(8,128)S(1)} %bitcast.620, f32[272]{0:T(512)S(1)} %fusion.241), kind=kOutput, calls=%fused_computation.5 | convolution fusion | flops 2784215040 | bytes 10404928 | tf_op jit(solution)/shard_map/rk,rd->kd/dot_general | solution.py:548
  238.0 6.2 %multiply_convert_fusion.2 = bf16[544,768]{1,0:T(8,128)(2,1)S(1)} fusion(f32[544,768]{1,0:T(8,128)S(1)} %copy-done.16, bf16[544,3072]{1,0:T(8,128)(2,1)} %get-tuple-element.129, bf16[3072,768]{1,0:T(8,128)(2,1)} %bitcast.567, f32[544]{0:T(1024)S(1)} %copy-done.51, f32[768]{0:T(1024)S(1)} %copy-done.77), kind=kOutput, calls=%fused_computation.46 | convolution fusion | flops 2568585216 | bytes 10572928 | tf_op jit(solution)/shard_map/dot_general | solution.py:606
  245.9 4.2 convolution_convert_fusion.1
  260.8 4.8 convolution_convert_fusion.2
  270.1 9.7 %fusion.11 = f32[2,1024,832]{1,2,0:T(8,128)} fusion(bf16[2,832,768]{2,1,0:T(8,128)(2,1)} %fusion, s32[2,272]{1,0:T(2,128)S(1)} %copy-done.69, f32[2,272,768]{2,1,0:T(8,128)} %bitcast.621, f32[272]{0:T(512)S(1)} %fusion.241), kind=kOutput, calls=%fused_computation.21 | convolution fusion | flops 3475849216 | bytes 11046080 | tf_op jit(solution)/shard_map/cpd,cvd->cpv/dot_general | solution.py:603
  292.1 9.2 %collective-permute-done.47 = bf16[2,2,24,3072]{3,2,1,0:T(8,128)(2,1)S(1)} collective-permute-done((bf16[2,2,24,3072]{3,2,1,0:T(8,128)(2,1)S(1)}, bf16[2,2,24,3072]{3,2,1,0:T(8,128)(2,1)S(1)}, u32[]{:S(2)}, u32[]{:S(2)}) %collective-permute-start.47) | collective-permute-done | bytes 589856 | tf_op jit(solution)/shard_map/ppermute | solution.py:43
  303.2 10.2 %collective-permute-done.46 = bf16[2,2,24,3072]{3,2,1,0:T(8,128)(2,1)S(1)} collective-permute-done((bf16[2,2,24,3072]{3,2,1,0:T(8,128)(2,1)S(1)}, bf16[2,2,24,3072]{3,2,1,0:T(8,128)(2,1)S(1)}, u32[]{:S(2)}, u32[]{:S(2)}) %collective-permute-start.46) | collective-permute-done | bytes 589856 | tf_op jit(solution)/shard_map/ppermute | solution.py:43
  319.8 20.6 %collective-permute-done.31 = bf16[2,2,104,768]{3,2,1,0:T(8,128)(2,1)S(1)} collective-permute-done((bf16[2,2,104,768]{3,2,1,0:T(8,128)(2,1)S(1)}, bf16[2,2,104,768]{3,2,1,0:T(8,128)(2,1)S(1)}, u32[]{:S(2)}, u32[]{:S(2)}) %collective-permute-start.31) | collective-permute-done | bytes 639008 | tf_op jit(solution)/shard_map/ppermute | solution.py:43
  352.0 7.3 %collective-permute-done.35 = bf16[104,768]{1,0:T(8,128)(2,1)S(1)} collective-permute-done((bf16[104,768]{1,0:T(8,128)(2,1)S(1)}, bf16[104,768]{1,0:T(8,128)(2,1)S(1)}, u32[]{:S(2)}, u32[]{:S(2)}) %collective-permute-start.35) | collective-permute-done | bytes 159776 | tf_op jit(solution)/shard_map/ppermute | solution.py:43
  398.8 19.5 %collective-permute-done.52 = bf16[2,2,24,6144]{3,2,1,0:T(8,128)(2,1)S(1)} collective-permute-done((bf16[2,2,24,6144]{3,2,1,0:T(8,128)(2,1)}, bf16[2,2,24,6144]{3,2,1,0:T(8,128)(2,1)S(1)}, u32[]{:S(2)}, u32[]{:S(2)}) %collective-permute-start.52) | collective-permute-done | bytes 1179680 | tf_op jit(solution)/shard_map/ppermute | solution.py:43
  418.4 5.7 %collective-permute-done.53 = bf16[2,2,24,6144]{3,2,1,0:T(8,128)(2,1)S(1)} collective-permute-done((bf16[2,2,24,6144]{3,2,1,0:T(8,128)(2,1)}, bf16[2,2,24,6144]{3,2,1,0:T(8,128)(2,1)S(1)}, u32[]{:S(2)}, u32[]{:S(2)}) %collective-permute-start.53) | collective-permute-done | bytes 1179680 | tf_op jit(solution)/shard_map/ppermute | solution.py:43
  424.2 23.6 %collective-permute-done.54 = bf16[2,2,24,6144]{3,2,1,0:T(8,128)(2,1)S(1)} collective-permute-done((bf16[2,2,24,6144]{3,2,1,0:T(8,128)(2,1)}, bf16[2,2,24,6144]{3,2,1,0:T(8,128)(2,1)S(1)}, u32[]{:S(2)}, u32[]{:S(2)}) %collective-permute-start.54) | collective-permute-done | bytes 1179680 | tf_op jit(solution)/shard_map/ppermute | solution.py:43
  465.7 7.9 %collective-permute-done.56 = bf16[24,6144]{1,0:T(8,128)(2,1)S(1)} collective-permute-done((bf16[24,6144]{1,0:T(8,128)(2,1)S(1)}, bf16[24,6144]{1,0:T(8,128)(2,1)S(1)}, u32[]{:S(2)}, u32[]{:S(2)}) %collective-permute-start.56) | collective-permute-done | bytes 294944 | tf_op jit(solution)/shard_map/ppermute | solution.py:43
  474.4 4.8 collective-permute-done.55
  (450 shorter events, 198.1 us)
Async XLA Ops:
  2.4 34.7 %collective-permute-start.12 = (bf16[1,24,3072]{2,1,0:T(8,128)(2,1)}, bf16[1,24,3072]{2,1,0:T(8,128)(2,1)}, u32[]{:S(2)}, u32[]{:S(2)}) collective-permute-start(bf16[1,24,3072]{2,1,0:T(8,128)(2,1)} %maximum_bitcast_fusion), channel_id=1, source_target_pairs={{0,24},{1,25},{2,26},{3,27},{4,28},{5,29},{6,30},{7,31},{8,16},{9,... | collective-permute-start | bytes 442376 | tf_op jit(solution)/shard_map/ppermute | solution.py:43
  7.5 30.3 %collective-permute-start.11 = (bf16[1,24,3072]{2,1,0:T(8,128)(2,1)}, bf16[1,24,3072]{2,1,0:T(8,128)(2,1)}, u32[]{:S(2)}, u32[]{:S(2)}) collective-permute-start(bf16[1,24,3072]{2,1,0:T(8,128)(2,1)} %maximum_bitcast_fusion), channel_id=1, source_target_pairs={{0,16},{1,17},{2,18},{3,19},{4,20},{5,21},{6,22},{7,23},{8,24},{9,... | collective-permute-start | bytes 442376 | tf_op jit(solution)/shard_map/ppermute | solution.py:43
  7.5 34.1 %collective-permute-start.10 = (bf16[1,24,3072]{2,1,0:T(8,128)(2,1)}, bf16[1,24,3072]{2,1,0:T(8,128)(2,1)}, u32[]{:S(2)}, u32[]{:S(2)}) collective-permute-start(bf16[1,24,3072]{2,1,0:T(8,128)(2,1)} %maximum_bitcast_fusion), channel_id=1, source_target_pairs={{0,8},{1,9},{2,10},{3,11},{4,12},{5,13},{6,14},{7,15},{8,0},{9,1},... | collective-permute-start | bytes 442376 | tf_op jit(solution)/shard_map/ppermute | solution.py:43
  16.3 26.5 %collective-permute-start.2 = (bf16[1,104,768]{2,1,0:T(8,128)(2,1)}, bf16[1,104,768]{2,1,0:T(8,128)(2,1)}, u32[]{:S(2)}, u32[]{:S(2)}) collective-permute-start(bf16[1,104,768]{2,1,0:T(8,128)(2,1)} %broadcast_in_dim_reshape.3), channel_id=1, source_target_pairs={{0,24},{1,25},{2,26},{3,27},{4,28},{5,29},{6,30},{7,31},{8,16},{9,... | collective-permute-start | bytes 479240 | tf_op jit(solution)/shard_map/ppermute | solution.py:43
  20.1 22.7 %collective-permute-start.1 = (bf16[1,104,768]{2,1,0:T(8,128)(2,1)}, bf16[1,104,768]{2,1,0:T(8,128)(2,1)}, u32[]{:S(2)}, u32[]{:S(2)}) collective-permute-start(bf16[1,104,768]{2,1,0:T(8,128)(2,1)} %broadcast_in_dim_reshape.3), channel_id=1, source_target_pairs={{0,16},{1,17},{2,18},{3,19},{4,20},{5,21},{6,22},{7,23},{8,24},{9,... | collective-permute-start | bytes 479240 | tf_op jit(solution)/shard_map/ppermute | solution.py:43
  41.6 23.6 %collective-permute-start.21 = (bf16[1,24,6144]{2,1,0:T(8,128)(2,1)}, bf16[1,24,6144]{2,1,0:T(8,128)(2,1)S(1)}, u32[]{:S(2)}, u32[]{:S(2)}) collective-permute-start(bf16[1,24,6144]{2,1,0:T(8,128)(2,1)} %bitcast.631), channel_id=1, source_target_pairs={{0,16},{1,17},{2,18},{3,19},{4,20},{5,21},{6,22},{7,23},{8,24},{9,... | collective-permute-start | bytes 884744 | tf_op jit(solution)/shard_map/ppermute | solution.py:43
  42.8 31.6 %collective-permute-start.16 = (bf16[4,24,3072]{2,1,0:T(8,128)(2,1)S(1)}, bf16[4,24,3072]{2,1,0:T(8,128)(2,1)S(1)}, u32[]{:S(2)}, u32[]{:S(2)}) collective-permute-start(bf16[4,24,3072]{2,1,0:T(8,128)(2,1)S(1)} %pad_maximum_fusion.2.refs_0_), channel_id=1, source_target_pairs={{0,2},{1,3},{2,0},{3,1},{4,6},{5,7},{6,4},{7,5},{8,10},{9,11},{10,... | collective-permute-start | bytes 1769480 | tf_op jit(solution)/shard_map/ppermute | solution.py:43
  42.9 32.8 %collective-permute-start.15 = (bf16[4,24,3072]{2,1,0:T(8,128)(2,1)S(1)}, bf16[4,24,3072]{2,1,0:T(8,128)(2,1)}, u32[]{:S(2)}, u32[]{:S(2)}) collective-permute-start(bf16[4,24,3072]{2,1,0:T(8,128)(2,1)S(1)} %pad_maximum_fusion.2.refs_0_), channel_id=1, source_target_pairs={{0,5},{1,4},{2,7},{3,6},{4,1},{5,0},{6,3},{7,2},{8,13},{9,12},{10,... | collective-permute-start | bytes 1769480 | tf_op jit(solution)/shard_map/ppermute | solution.py:43
  45.4 30.8 %collective-permute-start.14 = (bf16[4,24,3072]{2,1,0:T(8,128)(2,1)S(1)}, bf16[4,24,3072]{2,1,0:T(8,128)(2,1)}, u32[]{:S(2)}, u32[]{:S(2)}) collective-permute-start(bf16[4,24,3072]{2,1,0:T(8,128)(2,1)S(1)} %pad_maximum_fusion.2.refs_0_), channel_id=1, source_target_pairs={{0,4},{1,5},{2,6},{3,7},{4,0},{5,1},{6,2},{7,3},{8,12},{9,13},{10,... | collective-permute-start | bytes 1769480 | tf_op jit(solution)/shard_map/ppermute | solution.py:43
  53.1 23.1 %collective-permute-start.13 = (bf16[4,24,3072]{2,1,0:T(8,128)(2,1)S(1)}, bf16[4,24,3072]{2,1,0:T(8,128)(2,1)}, u32[]{:S(2)}, u32[]{:S(2)}) collective-permute-start(bf16[4,24,3072]{2,1,0:T(8,128)(2,1)S(1)} %pad_maximum_fusion.2.refs_0_), channel_id=1, source_target_pairs={{0,1},{1,0},{2,3},{3,2},{4,5},{5,4},{6,7},{7,6},{8,9},{9,8},{10,11... | collective-permute-start | bytes 1769480 | tf_op jit(solution)/shard_map/ppermute | solution.py:43
  75.2 24.8 %collective-permute-start.4 = (bf16[4,104,768]{2,1,0:T(8,128)(2,1)}, bf16[4,104,768]{2,1,0:T(8,128)(2,1)}, u32[]{:S(2)}, u32[]{:S(2)}) collective-permute-start(bf16[4,104,768]{2,1,0:T(8,128)(2,1)} %constant_dynamic-update-slice_fusion.refs_0_), channel_id=1, source_target_pairs={{0,4},{1,5},{2,6},{3,7},{4,0},{5,1},{6,2},{7,3},{8,12},{9,13},{10,... | collective-permute-start | bytes 1916936 | tf_op jit(solution)/shard_map/ppermute | solution.py:43
  75.7 24.3 %collective-permute-start.3 = (bf16[4,104,768]{2,1,0:T(8,128)(2,1)}, bf16[4,104,768]{2,1,0:T(8,128)(2,1)}, u32[]{:S(2)}, u32[]{:S(2)}) collective-permute-start(bf16[4,104,768]{2,1,0:T(8,128)(2,1)} %constant_dynamic-update-slice_fusion.refs_0_), channel_id=1, source_target_pairs={{0,1},{1,0},{2,3},{3,2},{4,5},{5,4},{6,7},{7,6},{8,9},{9,8},{10,11... | collective-permute-start | bytes 1916936 | tf_op jit(solution)/shard_map/ppermute | solution.py:43
  76.2 24.3 %collective-permute-start.19 = (bf16[4,24,3072]{2,1,0:T(8,128)(2,1)}, bf16[4,24,3072]{2,1,0:T(8,128)(2,1)}, u32[]{:S(2)}, u32[]{:S(2)}) collective-permute-start(bf16[4,24,3072]{2,1,0:T(8,128)(2,1)} %collective-permute-done.15.refs_3_), channel_id=1, source_target_pairs={{0,2},{1,3},{2,0},{3,1},{4,6},{5,7},{6,4},{7,5},{8,10},{9,11},{10,... | collective-permute-start | bytes 1769480 | tf_op jit(solution)/shard_map/ppermute | solution.py:43
  76.2 24.3 %collective-permute-start.18 = (bf16[4,24,3072]{2,1,0:T(8,128)(2,1)}, bf16[4,24,3072]{2,1,0:T(8,128)(2,1)}, u32[]{:S(2)}, u32[]{:S(2)}) collective-permute-start(bf16[4,24,3072]{2,1,0:T(8,128)(2,1)} %collective-permute-done.14.refs_2_), channel_id=1, source_target_pairs={{0,2},{1,3},{2,0},{3,1},{4,6},{5,7},{6,4},{7,5},{8,10},{9,11},{10,... | collective-permute-start | bytes 1769480 | tf_op jit(solution)/shard_map/ppermute | solution.py:43
  102.4 72.9 %collective-permute-start.26 = (bf16[4,24,6144]{2,1,0:T(8,128)(2,1)S(1)}, bf16[4,24,6144]{2,1,0:T(8,128)(2,1)S(1)}, u32[]{:S(2)}, u32[]{:S(2)}) collective-permute-start(bf16[4,24,6144]{2,1,0:T(8,128)(2,1)S(1)} %pad_maximum_fusion.1.refs_0_), channel_id=1, source_target_pairs={{0,2},{1,3},{2,0},{3,1},{4,6},{5,7},{6,4},{7,5},{8,10},{9,11},{10,... | collective-permute-start | bytes 3538952 | tf_op jit(solution)/shard_map/ppermute | solution.py:43
  109.2 40.5 %collective-permute-start.25 = (bf16[4,24,6144]{2,1,0:T(8,128)(2,1)S(1)}, bf16[4,24,6144]{2,1,0:T(8,128)(2,1)S(1)}, u32[]{:S(2)}, u32[]{:S(2)}) collective-permute-start(bf16[4,24,6144]{2,1,0:T(8,128)(2,1)S(1)} %pad_maximum_fusion.1.refs_0_), channel_id=1, source_target_pairs={{0,5},{1,4},{2,7},{3,6},{4,1},{5,0},{6,3},{7,2},{8,13},{9,12},{10,... | collective-permute-start | bytes 3538952 | tf_op jit(solution)/shard_map/ppermute | solution.py:43
  111.5 51.9 %collective-permute-start.24 = (bf16[4,24,6144]{2,1,0:T(8,128)(2,1)S(1)}, bf16[4,24,6144]{2,1,0:T(8,128)(2,1)}, u32[]{:S(2)}, u32[]{:S(2)}) collective-permute-start(bf16[4,24,6144]{2,1,0:T(8,128)(2,1)S(1)} %pad_maximum_fusion.1.refs_0_), channel_id=1, source_target_pairs={{0,4},{1,5},{2,6},{3,7},{4,0},{5,1},{6,2},{7,3},{8,12},{9,13},{10,... | collective-permute-start | bytes 3538952 | tf_op jit(solution)/shard_map/ppermute | solution.py:43
  112.1 51.8 %collective-permute-start.23 = (bf16[4,24,6144]{2,1,0:T(8,128)(2,1)S(1)}, bf16[4,24,6144]{2,1,0:T(8,128)(2,1)}, u32[]{:S(2)}, u32[]{:S(2)}) collective-permute-start(bf16[4,24,6144]{2,1,0:T(8,128)(2,1)S(1)} %pad_maximum_fusion.1.refs_0_), channel_id=1, source_target_pairs={{0,1},{1,0},{2,3},{3,2},{4,5},{5,4},{6,7},{7,6},{8,9},{9,8},{10,11... | collective-permute-start | bytes 3538952 | tf_op jit(solution)/shard_map/ppermute | solution.py:43
  149.7 25.6 %collective-permute-start.29 = (bf16[4,24,6144]{2,1,0:T(8,128)(2,1)S(1)}, bf16[4,24,6144]{2,1,0:T(8,128)(2,1)S(1)}, u32[]{:S(2)}, u32[]{:S(2)}) collective-permute-start(bf16[4,24,6144]{2,1,0:T(8,128)(2,1)S(1)} %collective-permute-done.25.refs_3_), channel_id=1, source_target_pairs={{0,2},{1,3},{2,0},{3,1},{4,6},{5,7},{6,4},{7,5},{8,10},{9,11},{10,... | collective-permute-start | bytes 3538952 | tf_op jit(solution)/shard_map/ppermute | solution.py:43
  252.1 27.8 %collective-permute-start.44 = (bf16[2,2,2,2,24,3072]{5,4,3,2,1,0:T(8,128)(2,1)}, bf16[2,2,2,2,24,3072]{5,4,3,2,1,0:T(8,128)(2,1)}, u32[]{:S(2)}, u32[]{:S(2)}) collective-permute-start(bf16[2,2,2,2,24,3072]{5,4,3,2,1,0:T(8,128)(2,1)} %pad_maximum_fusion), channel_id=1, source_target_pairs={{0,2},{1,3},{2,0},{3,1},{4,6},{5,7},{6,4},{7,5},{8,10},{9,11},{10,... | collective-permute-start | bytes 7077896 | tf_op jit(solution)/shard_map/ppermute | solution.py:43
  256.6 32.5 %collective-permute-start.30 = (bf16[2,2,2,2,104,768]{5,4,3,2,1,0:T(8,128)(2,1)}, bf16[2,2,2,2,104,768]{5,4,3,2,1,0:T(8,128)(2,1)}, u32[]{:S(2)}, u32[]{:S(2)}) collective-permute-start(bf16[2,2,2,2,104,768]{5,4,3,2,1,0:T(8,128)(2,1)} %dynamic-slice_bitcast_fusion), channel_id=1, source_target_pairs={{0,2},{1,3},{2,0},{3,1},{4,6},{5,7},{6,4},{7,5},{8,10},{9,11},{10,... | collective-permute-start | bytes 7667720 | tf_op jit(solution)/shard_map/ppermute | solution.py:43
  268.5 111.1 %collective-permute-start.51 = (bf16[2,2,2,2,24,6144]{5,4,3,2,1,0:T(8,128)(2,1)}, bf16[2,2,2,2,24,6144]{5,4,3,2,1,0:T(8,128)(2,1)}, u32[]{:S(2)}, u32[]{:S(2)}) collective-permute-start(bf16[2,2,2,2,24,6144]{5,4,3,2,1,0:T(8,128)(2,1)} %bitcast_dynamic-update-slice_fusion), channel_id=1, source_target_pairs={{0,2},{1,3},{2,0},{3,1},{4,6},{5,7},{6,4},{7,5},{8,10},{9,11},{10,... | collective-permute-start | bytes 14155784 | tf_op jit(solution)/shard_map/ppermute | solution.py:43
  286.1 27.3 %collective-permute-start.46 = (bf16[2,2,24,3072]{3,2,1,0:T(8,128)(2,1)S(1)}, bf16[2,2,24,3072]{3,2,1,0:T(8,128)(2,1)S(1)}, u32[]{:S(2)}, u32[]{:S(2)}) collective-permute-start(bf16[2,2,24,3072]{3,2,1,0:T(8,128)(2,1)S(1)} %pad_maximum_fusion.4), channel_id=1, source_target_pairs={{0,4},{1,5},{2,6},{3,7},{4,0},{5,1},{6,2},{7,3},{8,12},{9,13},{10,... | collective-permute-start | bytes 1769480 | tf_op jit(solution)/shard_map/ppermute | solution.py:43
  286.8 28.2 %collective-permute-start.45 = (bf16[2,2,24,3072]{3,2,1,0:T(8,128)(2,1)S(1)}, bf16[2,2,24,3072]{3,2,1,0:T(8,128)(2,1)S(1)}, u32[]{:S(2)}, u32[]{:S(2)}) collective-permute-start(bf16[2,2,24,3072]{3,2,1,0:T(8,128)(2,1)S(1)} %pad_maximum_fusion.3), channel_id=1, source_target_pairs={{0,1},{1,0},{2,3},{3,2},{4,5},{5,4},{6,7},{7,6},{8,9},{9,8},{10,11... | collective-permute-start | bytes 1769480 | tf_op jit(solution)/shard_map/ppermute | solution.py:43
  291.1 49.3 %collective-permute-start.31 = (bf16[2,2,104,768]{3,2,1,0:T(8,128)(2,1)S(1)}, bf16[2,2,104,768]{3,2,1,0:T(8,128)(2,1)S(1)}, u32[]{:S(2)}, u32[]{:S(2)}) collective-permute-start(bf16[2,2,104,768]{3,2,1,0:T(8,128)(2,1)S(1)} %get-tuple-element.52), channel_id=1, source_target_pairs={{0,1},{1,0},{2,3},{3,2},{4,5},{5,4},{6,7},{7,6},{8,9},{9,8},{10,11... | collective-permute-start | bytes 1916936 | tf_op jit(solution)/shard_map/ppermute | solution.py:43
  301.3 39.7 %collective-permute-start.33 = (bf16[2,2,104,768]{3,2,1,0:T(8,128)(2,1)S(1)}, bf16[2,2,104,768]{3,2,1,0:T(8,128)(2,1)S(1)}, u32[]{:S(2)}, u32[]{:S(2)}) collective-permute-start(bf16[2,2,104,768]{3,2,1,0:T(8,128)(2,1)S(1)} %get-tuple-element.53), channel_id=1, source_target_pairs={{0,5},{1,4},{2,7},{3,6},{4,1},{5,0},{6,3},{7,2},{8,13},{9,12},{10,... | collective-permute-start | bytes 1916936 | tf_op jit(solution)/shard_map/ppermute | solution.py:43
  313.5 30.2 %collective-permute-start.32 = (bf16[2,2,104,768]{3,2,1,0:T(8,128)(2,1)S(1)}, bf16[2,2,104,768]{3,2,1,0:T(8,128)(2,1)S(1)}, u32[]{:S(2)}, u32[]{:S(2)}) collective-permute-start(bf16[2,2,104,768]{3,2,1,0:T(8,128)(2,1)S(1)} %get-tuple-element.54), channel_id=1, source_target_pairs={{0,4},{1,5},{2,6},{3,7},{4,0},{5,1},{6,2},{7,3},{8,12},{9,13},{10,... | collective-permute-start | bytes 1916936 | tf_op jit(solution)/shard_map/ppermute | solution.py:43
  316.1 30.1 %collective-permute-start.50 = (bf16[24,3072]{1,0:T(8,128)(2,1)S(1)}, bf16[24,3072]{1,0:T(8,128)(2,1)S(1)}, u32[]{:S(2)}, u32[]{:S(2)}) collective-permute-start(bf16[24,3072]{1,0:T(8,128)(2,1)S(1)} %pad_maximum_fusion.9), channel_id=1, source_target_pairs={{0,24},{1,25},{2,26},{3,27},{4,28},{5,29},{6,30},{7,31},{8,16},{9,... | collective-permute-start | bytes 442376 | tf_op jit(solution)/shard_map/ppermute | solution.py:43
  390.8 27.5 %collective-permute-start.52 = (bf16[2,2,24,6144]{3,2,1,0:T(8,128)(2,1)}, bf16[2,2,24,6144]{3,2,1,0:T(8,128)(2,1)S(1)}, u32[]{:S(2)}, u32[]{:S(2)}) collective-permute-start(bf16[2,2,24,6144]{3,2,1,0:T(8,128)(2,1)} %get-tuple-element.61), channel_id=1, source_target_pairs={{0,1},{1,0},{2,3},{3,2},{4,5},{5,4},{6,7},{7,6},{8,9},{9,8},{10,11... | collective-permute-start | bytes 3538952 | tf_op jit(solution)/shard_map/ppermute | solution.py:43
  395.0 29.1 %collective-permute-start.53 = (bf16[2,2,24,6144]{3,2,1,0:T(8,128)(2,1)}, bf16[2,2,24,6144]{3,2,1,0:T(8,128)(2,1)S(1)}, u32[]{:S(2)}, u32[]{:S(2)}) collective-permute-start(bf16[2,2,24,6144]{3,2,1,0:T(8,128)(2,1)} %get-tuple-element.62), channel_id=1, source_target_pairs={{0,4},{1,5},{2,6},{3,7},{4,0},{5,1},{6,2},{7,3},{8,12},{9,13},{10,... | collective-permute-start | bytes 3538952 | tf_op jit(solution)/shard_map/ppermute | solution.py:43
  396.5 51.4 %collective-permute-start.54 = (bf16[2,2,24,6144]{3,2,1,0:T(8,128)(2,1)}, bf16[2,2,24,6144]{3,2,1,0:T(8,128)(2,1)S(1)}, u32[]{:S(2)}, u32[]{:S(2)}) collective-permute-start(bf16[2,2,24,6144]{3,2,1,0:T(8,128)(2,1)} %copy-done.50), channel_id=1, source_target_pairs={{0,5},{1,4},{2,7},{3,6},{4,1},{5,0},{6,3},{7,2},{8,13},{9,12},{10,... | collective-permute-start | bytes 3538952 | tf_op jit(solution)/shard_map/ppermute | solution.py:43
  452.2 21.4 %collective-permute-start.56 = (bf16[24,6144]{1,0:T(8,128)(2,1)S(1)}, bf16[24,6144]{1,0:T(8,128)(2,1)S(1)}, u32[]{:S(2)}, u32[]{:S(2)}) collective-permute-start(bf16[24,6144]{1,0:T(8,128)(2,1)S(1)} %fusion.115), channel_id=1, source_target_pairs={{0,16},{1,17},{2,18},{3,19},{4,20},{5,21},{6,22},{7,23},{8,24},{9,... | collective-permute-start | bytes 884744 | tf_op jit(solution)/shard_map/ppermute | solution.py:43
  (115 other events, 1294.3 us)

commit v2 on v1

--- a/solution.py
+++ b/solution.py
@@ -43,153 +43,489 @@
     return lax.ppermute(values, AXES, [(i, i ^ mask) for i in range(count)])
 
 
-def place_kernel(offsets, splits, index_ref, *refs):
+def window(ref, first, rows, start, width):
+    if rows != ref.shape[-2]:
+        ref = ref.at[(slice(None),) * (len(ref.shape) - 2) + (pl.ds(first, rows),)]
+    if width != ref.shape[-1]:
+        ref = ref.at[(slice(None),) * (len(ref.shape) - 1) + (pl.ds(start, width),)]
+    return ref
+
+
+def place_kernel(offsets, part, splits, index_ref, *refs):
     pieces, refs = refs[: len(offsets)], refs[len(offsets) :]
-    outs, refs = refs[: 1 + max(s[0] for s in splits)], refs[1 + max(s[0] for s in splits) :]
-    staged, in_sems, out_sems = refs
-    me = index_ref[0]
-    arrivals, departures = [], []
-    first = 0
+    outs, (staged, in_sems, out_sems) = refs[:-3], refs[-3:]
+    arrive, depart = placing(
+        offsets, part, splits, index_ref[0], pieces, outs, staged, in_sems, out_sems
+    )
+    arrive()
+    depart()()
+
+
+def placing(offsets, part, splits, me, pieces, outs, staged, in_sems, out_sems):
+    arrivals, first = [], 0
     for i, piece in enumerate(pieces):
         size = piece.shape[0]
         arrivals.append(
-            pltpu.make_async_copy(piece, staged.at[pl.ds(first, size)], in_sems.at[i])
-        )
-        arrivals[-1].start()
+            pltpu.make_async_copy(
+                window(piece, *part, 0, piece.shape[-1]),
+                staged.at[pl.ds(first, size)],
+                in_sems.at[i],
+            )
+        )
         first += size
-    first = 0
-    for arrival, masks in zip(arrivals, offsets):
-        arrival.wait()
-        for t, mask in enumerate(masks):
-            for which, slot, start, size in splits:
-                target = outs[which].at[me ^ mask]
-                departures.append(
-                    pltpu.make_async_copy(
-                        staged.at[first + t, :, pl.ds(start, size)],
-                        target if slot is None else target.at[slot],
-                        out_sems.at[len(departures)],
+
+    def arrive():
+        for arrival in arrivals:
+            arrival.start()
+
+    def depart():
+        departures, first = [], 0
+        for arrival, masks in zip(arrivals, offsets):
+            arrival.wait()
+            for t, mask in enumerate(masks):
+                for which, slot, row, rows, start, width, at in splits:
+                    target = outs[which].at[me ^ mask]
+                    target = target if slot is None else target.at[slot]
+                    source = staged.at[first + t]
+                    departures.append(
+                        pltpu.make_async_copy(
+                            window(source, row, rows, start, width),
+                            window(target, 0, rows, at, width),
+                            out_sems.at[len(departures)],
+                        )
                     )
-                )
-                departures[-1].start()
-        first += len(masks)
-    for departure in departures:
-        departure.wait()
-
-
-def place(pieces, masks, splits, shapes, index, count):
-    kind = pieces[0].dtype
-    row = pieces[0].shape[1:]
+                    departures[-1].start()
+            first += len(masks)
+
+        def wait():
+            for departure in departures:
+                departure.wait()
+
+        return wait
+
+    return arrive, depart
+
+
+def place(pieces, masks, part, splits, shapes, index, count):
+    kind, width = pieces[0].dtype, pieces[0].shape[-1]
     return pl.pallas_call(
-        functools.partial(place_kernel, masks, splits),
+        functools.partial(place_kernel, masks, part, splits),
         out_shape=[jax.ShapeDtypeStruct((count, *s), kind) for s in shapes],
         in_specs=[pl.BlockSpec(memory_space=pltpu.SMEM)]
         + [pl.BlockSpec(memory_space=pl.ANY)] * len(pieces),
         out_specs=[pl.BlockSpec(memory_space=pl.ANY)] * len(shapes),
         scratch_shapes=[
-            pltpu.VMEM((count, *row), kind),
+            pltpu.VMEM((count, part[1], width), kind),
             pltpu.SemaphoreType.DMA((len(pieces),)),
             pltpu.SemaphoreType.DMA((count * len(splits),)),
         ],
         compiler_params=pltpu.CompilerParams(vmem_limit_bytes=32 * 2**20),
         cost_estimate=pl.CostEstimate(
             flops=0,
-            bytes_accessed=4 * count * math.prod(row),
+            bytes_accessed=4 * count * part[1] * width,
             transcendentals=0,
         ),
         name="place",
     )(index, *pieces)
 
 
-def gather(shards, index, count):
-    rows = min(s.shape[0] for s in shards)
-    columns, splits, shapes = [], [], []
-    start = 0
-    for which, shard in enumerate(shards):
-        parts = shard.shape[0] // rows
-        shapes.append((parts, rows, shard.shape[1]) if parts > 1 else (rows, shard.shape[1]))
-        for i in range(parts):
-            columns.append(shard[i * rows : (i + 1) * rows])
-            splits.append((which, i if parts > 1 else None, start, shard.shape[1]))
-            start += shard.shape[1]
-    groups = bit_groups(count)
-    data, masks = jnp.concatenate(columns, axis=1)[None], [0]
-    for group in groups[:-2]:
-        ours = masks_of(group)
-        data = jnp.concatenate(
-            [data] + [swap(data, m, count) for m in ours[1:]], axis=0
-        )
-        masks = [m ^ q for m in ours for q in masks]
-    pieces = [(masks, data)]
-    for group in groups[-2:]:
-        pieces = pieces + [
-            ([m ^ q for q in held], swap(piece, m, count))
-            for m in masks_of(group)[1:]
-            for held, piece in pieces
+def stack_kernel(sizes, *refs):
+    total = sum(sizes)
+    pieces, outs = refs[:total], refs[total : total + len(sizes)]
+    staged, sems = refs[total + len(sizes) : -1], refs[-1]
+    arrivals, done = [], 0
+    for buffer, size in zip(staged, sizes):
+        for i, piece in enumerate(pieces[done : done + size]):
+            arrivals.append(
+                pltpu.make_async_copy(
+                    piece,
+                    buffer.at[pl.ds(i * piece.shape[0], piece.shape[0])],
+                    sems.at[done + i],
+                )
+            )
+        done += size
+    for arrival in arrivals:
+        arrival.start()
+    departures, done = [], 0
+    for o, (buffer, size) in enumerate(zip(staged, sizes)):
+        for arrival in arrivals[done : done + size]:
+            arrival.wait()
+        done += size
+        departures.append(
+            pltpu.make_async_copy(buffer, outs[o], sems.at[total + o])
+        )
+        departures[-1].start()
+    for departure in departures:
+        departure.wait()
+
+
+def stack(groups):
+    pieces = [p for group in groups for p in group]
+    kind, tail = pieces[0].dtype, pieces[0].shape[1:]
+    shapes = [(sum(p.shape[0] for p in g), *tail) for g in groups]
+    return pl.pallas_call(
+        functools.partial(stack_kernel, [len(g) for g in groups]),
+        out_shape=[jax.ShapeDtypeStruct(s, kind) for s in shapes],
+        in_specs=[pl.BlockSpec(memory_space=pl.ANY)] * len(pieces),
+        out_specs=[pl.BlockSpec(memory_space=pl.ANY)] * len(groups),
+        scratch_shapes=[pltpu.VMEM(s, kind) for s in shapes]
+        + [pltpu.SemaphoreType.DMA((len(pieces) + len(groups),))],
+        cost_estimate=pl.CostEstimate(
+            flops=0,
+            bytes_accessed=4 * sum(math.prod(s) for s in shapes),
+            transcendentals=0,
+        ),
+        name="stack",
+    )(*pieces)
+
+
+def join_kernel(parts, *refs):
+    arrays, (out, staged, sems) = refs[:-3], refs[-3:]
+    copies = []
+    for which, row, rows, start, width, to_row, to_start in parts:
+        copies.append(
+            pltpu.make_async_copy(
+                window(arrays[which], row, rows, start, width),
+                window(staged, to_row, rows, to_start, width),
+                sems.at[len(copies)],
+            )
+        )
+        copies[-1].start()
+    for copy in copies:
+        copy.wait()
+    back = pltpu.make_async_copy(staged, out, sems.at[len(parts)])
+    back.start()
+    back.wait()
+
+
+def join(arrays, parts, shape):
+    kind = arrays[0].dtype
+    return pl.pallas_call(
+        functools.partial(join_kernel, parts),
+        out_shape=jax.ShapeDtypeStruct(shape, kind),
+        in_specs=[pl.BlockSpec(memory_space=pl.ANY)] * len(arrays),
+        out_specs=pl.BlockSpec(memory_space=pl.ANY),
+        scratch_shapes=[
+            pltpu.VMEM(shape, kind),
+            pltpu.SemaphoreType.DMA((len(parts) + 1,)),
+        ],
+        name="join",
+    )(*arrays)
+
+
+class Layout:
+    def __init__(self, shards, width):
+        rows = min(s.shape[0] for s in shards)
+        self.by_rows = width is not None
+        self.parts, self.splits, self.shapes, self.shards = [], [], [], shards
+        row, column = 0, 0
+        for which, shard in enumerate(shards):
+            step = width if self.by_rows else shard.shape[1]
+            k = 1 if self.by_rows else shard.shape[0] // rows
+            size = shard.shape[0] // k
+            self.shapes.append((k, size, shard.shape[1]) if k > 1 else shard.shape)
+            for i in range(k):
+                for start in range(0, shard.shape[1], step):
+                    self.parts.append((which, i * size, size, start, step, row, column))
+                    self.splits.append(
+                        (which, i if k > 1 else None, row, size, column, step, start)
+                    )
+                    if self.by_rows:
+                        row += size
+                    else:
+                        column += step
+        self.shape = (row, width) if self.by_rows else (rows, column)
+
+    def joined(self):
+        if len(self.parts) == 1:
+            return self.shards[0]
+        if not self.by_rows:
+            return jnp.concatenate(
+                [
+                    self.shards[which][row : row + size]
+                    for which, row, size, *_ in self.parts
+                ],
+                axis=1,
+            )
+        return join(self.shards, self.parts, self.shape)
+
+
+def after(value, *others):
+    return lax.optimization_barrier((value, *others))[0]
+
+
+Y, CORE, X, Z0 = 1, 2, 4, 8
+
+
+class Gather:
+    def __init__(self, layout, index, count):
+        self.layout, self.index, self.count = layout, index, count
+        self.data = layout.joined()
+
+    def along_z(self, *others):
+        data, masks = after(self.data, *others)[None], [0]
+        for b in range(self.count.bit_length() - 2, 3, -1):
+            data = stack([[data, swap(data, 1 << b, self.count)]])[0]
+            masks = masks + [m ^ (1 << b) for m in masks]
+        self.first, self.masks, self.zs = data, masks, [data]
+        self.second = swap(data, Z0, self.count)
+        return self.second
+
+    def first_xy(self, *others):
+        first = after(self.first, *others)
+        self.by_y = swap(first, Y, self.count)
+        self.by_x = swap(after(self.second, *others), X, self.count)
+
+    def second_xy(self, *others):
+        masks = self.masks
+        by_y = after(self.by_y, *others)
+        (first, second) = stack([[self.first, by_y], [self.second, self.by_x]])
+        self.turn = first
+        of_first = masks + [m ^ Y for m in masks]
+        of_second = [m ^ Z0 for m in masks + [m ^ X for m in masks]]
+        self.pieces = [
+            (of_first, first),
+            (of_second, second),
+            ([m ^ X for m in of_first], swap(first, X, self.count)),
+            ([m ^ Y for m in of_second], swap(second, Y, self.count)),
         ]
-    wholes = place(
-        [p for _, p in pieces], [m for m, _ in pieces], splits, shapes, index, count
-    )
-    return [w.reshape(-1, w.shape[-1]) for w in wholes]
-
-
-def chosen_half(values, bits, group, mask, index):
-    starts, sizes, shape = [], [], []
-    for b in bits:
-        if b in group:
-            starts.append(((index[0] ^ mask) >> b) & 1)
-            sizes.append(1)
+        return [p for _, p in self.pieces[2:]]
+
+    def along_core(self, *others):
+        self.pieces = self.pieces + [
+            ([m ^ CORE for m in held], swap(after(piece, *others), CORE, self.count))
+            for held, piece in self.pieces
+        ]
+
+    def finish(self):
+        wholes = place(
+            [p for _, p in self.pieces],
+            [m for m, _ in self.pieces],
+            (0, self.layout.shape[0]),
+            self.layout.splits,
+            self.layout.shapes,
+            self.index,
+            self.count,
+        )
+        return [w.reshape(-1, w.shape[-1]) for w in wholes]
+
+
+def add_kernel(outs_of, index_ref, *refs):
+    outs = refs[len(refs) - len(outs_of) :]
+    for out, sources in zip(outs, outs_of):
+        for first, width, members in sources:
+            step = 768 if width % 768 == 0 else width
+            for at in range(0, width, step):
+                total = None
+                for which in members:
+                    value = refs[which][0, :, at : at + step].astype(SINGLE)
+                    total = value if total is None else total + value
+                out[0, :, first + at : first + at + step] = total.astype(out.dtype)
+
+
+def added(outputs, length, pieces, index, name):
+    in_specs, operands, outs_of, out_shape = [], [], [], []
+    for (low, high), kind, sources in outputs:
+        rows = sources[0][0].shape[1]
+        plan = []
+        for start, width in pieces:
+            if not low <= start < high:
+                continue
+            members = []
+            for array, first, where in sources:
+                if not first <= start < first + array.shape[2]:
+                    continue
+                at = (start - first) // width
+                assert at * width == start - first
+                in_specs.append(
+                    pl.BlockSpec(
+                        (1, rows, width),
+                        lambda h, ref, where=where, at=at: (where(ref[0], h), 0, at),
+                    )
+                )
+                members.append(len(operands))
+                operands.append(array)
+            plan.append((start - low, width, members))
+        outs_of.append(plan)
+        out_shape.append(jax.ShapeDtypeStruct((length, rows, high - low), kind))
+    moved = sum(length * math.prod(spec.block_shape) for spec in in_specs)
+    return pl.pallas_call(
+        functools.partial(add_kernel, outs_of),
+        out_shape=out_shape,
+        grid_spec=pltpu.PrefetchScalarGridSpec(
+            num_scalar_prefetch=1,
+            grid=(length,),
+            in_specs=in_specs,
+            out_specs=[
+                pl.BlockSpec((1, *s.shape[1:]), lambda h, ref: (h, 0, 0))
+                for s in out_shape
+            ],
+        ),
+        compiler_params=pltpu.CompilerParams(vmem_limit_bytes=32 * 2**20),
+        cost_estimate=pl.CostEstimate(
+            flops=moved, bytes_accessed=4 * moved, transcendentals=0
+        ),
+        name=name,
+    )(index, *[pltpu.with_memory_space_constraint(a, pltpu.HBM) for a in operands])
+
+
+def position(mask, count):
+    top = count.bit_length() - 2
+    high = 0
+    for j in range(top - 3):
+        high = high | (((mask >> (top - j)) & 1) << j)
+    z, x, c, y = (mask >> 3) & 1, (mask >> 2) & 1, (mask >> 1) & 1, mask & 1
+    inner, outer = z * x + (1 - z) * y, z * y + (1 - z) * x
+    return ((c * 4 + z + 2 * outer) << (top - 2)) + (inner << (top - 3)) + high
+
+
+class Scatter:
+    def __init__(self, count, index, relative=False):
+        self.count, self.index, self.relative = count, index, relative
+        self.own, self.cores, self.pieces, self.width = [], [], [], 0
+
+    def along_core(self, whole, *others):
+        rows, width = whole.shape[0] // self.count, whole.shape[1]
+        view = whole.reshape(self.count // 4, 2, 2, rows, width)
+        other = 1 - ((self.index[0] >> 1) & 1)
+        sending = lax.dynamic_slice_in_dim(view, other, 1, axis=1)
+        sending = sending.reshape(self.count // 2, rows, width)
+        return self.with_core(whole.reshape(self.count, rows, width), sending, *others)
+
+    def with_core(self, own, sending, *others):
+        self.sent = [after(sending, *others)]
+        self.own.append((own, self.width))
+        self.cores.append((swap(self.sent[0], CORE, self.count), self.width))
+        self.pieces.append((self.width, own.shape[2]))
+        self.width += own.shape[2]
+        return self
+
+    def sources(self, target, extra):
+        if self.relative:
+            both = lambda me, h: position(target(me, h) ^ me, self.count)
+            without = both
         else:
-            starts.append(0)
-            sizes.append(2)
-            shape.append(2)
-    tail = values.shape[len(bits) :]
-    zeros = [0] * len(tail)
-    return lax.dynamic_slice(values, starts + zeros, sizes + list(tail)).reshape(
-        *shape, *tail
-    )
-
-
-def scatter(wholes, index, count):
-    bits = list(range(count.bit_length() - 2, -1, -1))
-    rows = min(w.shape[0] for w in wholes) // count
-    kind = wholes[0].dtype
-    views, columns, start = [], [], 0
-    for whole in wholes:
-        k = whole.shape[0] // count // rows
-        view = whole.reshape([2] * len(bits) + [k, rows, whole.shape[1]])
-        for i in range(k):
-            columns.append((len(views), i, start, whole.shape[1]))
-            start += whole.shape[1]
-        views.append(view)
-    received = []
-    done = []
-
-    def part(mask):
-        pieces = []
-        own = [chosen_half(v, bits, done, mask, index) for v in views]
-        others = [chosen_half(v, left, done, mask, index) for v, left in received]
-        for which, i, first, width in columns:
-            piece = own[which][..., i, :, :]
-            if others:
-                piece = piece.astype(SINGLE)
-                for other in others:
-                    piece = piece + other[..., first : first + width].astype(SINGLE)
-            pieces.append(piece)
-        return pieces
-
-    for group in reversed(bit_groups(count)):
-        done = done + group
-        arrived = []
-        for m in masks_of(group)[1:]:
-            sent = jnp.concatenate([p.astype(kind) for p in part(m)], axis=-1)
-            arrived.append((swap(sent, m, count), [b for b in bits if b not in done]))
-        received = received + arrived
-    pieces = part(0)
-    out = []
-    for which in range(len(views)):
-        mine = [p for p, c in zip(pieces, columns) if c[0] == which]
-        out.append(jnp.concatenate(mine, axis=0) if len(mine) > 1 else mine[0])
-    return out
+            both = lambda me, h: target(me, h)
+            without = lambda me, h: ((target(me, h) >> 2) << 1) | (target(me, h) & 1)
+        return (
+            [(a, f, both) for a, f in self.own]
+            + [(a, f, without) for a, f in self.cores]
+            + [(a, 0, lambda me, h, at=at: at(h)) for a, at in extra]
+        )
+
+    def sums(self, targets, length, name):
+        kind = self.own[0][0].dtype
+        return added(
+            [((0, self.width), kind, self.sources(t, e)) for t, e in targets],
+            length,
+            self.pieces,
+            self.index,
+            name,
+        )
+
+    def first_xy(self, *others):
+        self.cores = [(after(a, *others), f) for a, f in self.cores]
+        to_x, to_y = self.sent = self.sums(
+            [
+                (lambda me, h: me ^ X ^ (h & 1) ^ ((h >> 1) << 4), []),
+                (lambda me, h: me ^ (Y | Z0) ^ ((h & 1) << 2) ^ ((h >> 1) << 4), []),
+            ],
+            2 * (self.count // 16),
+            "add_xy",
+        )
+        self.by_x, self.by_y = swap(to_x, X, self.count), swap(to_y, Y, self.count)
+        return self
+
+    def second_xy(self, *others):
+        by_x, by_y = after(self.by_x, *others), self.by_y
+        to_y, to_x = self.sent = self.sums(
+            [
+                (lambda me, h: me ^ Y ^ (h << 4), [(by_x, lambda h: 1 + 2 * h)]),
+                (lambda me, h: me ^ (X | Z0) ^ (h << 4), [(by_y, lambda h: 1 + 2 * h)]),
+            ],
+            self.count // 16,
+            "add_yx",
+        )
+        self.mine = [
+            (by_x, lambda h: 2 * h),
+            (swap(to_y, Y, self.count), lambda h: h),
+        ]
+        self.next = [
+            (by_y, lambda h: 2 * h),
+            (swap(to_x, X, self.count), lambda h: h),
+        ]
+        return self
+
+    def across_z(self, *others):
+        last, where = self.next[1]
+        extra = [self.next[0], (after(last, *others), where)]
+        self.sent = self.sums(
+            [(lambda me, h: me ^ Z0 ^ (h << 4), extra)], self.count // 16, "add_z"
+        )
+        self.mine.append((swap(self.sent[0], Z0, self.count), lambda h: h))
+        return self
+
+    def across_rest(self, *others):
+        last, where = self.mine[-1]
+        self.mine[-1] = (after(last, *others), where)
+        for b in range(self.count.bit_length() - 2, 3, -1):
+            far = 1 << (b - 4)
+            moved = [(a, lambda h, at=at, far=far: at(h + far)) for a, at in self.mine]
+            self.sent = self.sums(
+                [(lambda me, h, b=b: me ^ (1 << b) ^ (h << 4), moved)], far, "add_far"
+            )
+            self.mine.append((swap(self.sent[0], 1 << b, self.count), lambda h: h))
+        return self
+
+    def finish(self, *others):
+        last, where = self.mine[-1]
+        extra = self.mine[:-1] + [(after(last, *others), where)]
+        sources = self.sources(lambda me, h: me + h, extra)
+        totals = added(
+            [((f, f + a.shape[2]), SINGLE, sources) for a, f in self.own],
+            1,
+            self.pieces,
+            self.index,
+            "add_last",
+        )
+        return [t[0] for t in totals]
+
+
+def pack_rows(arrays, square, width):
+    blocks = width // square.shape[1]
+    rows = -(-square.shape[0] // (8 * blocks)) * 8
+    square = jnp.pad(square, ((0, rows * blocks - square.shape[0]), (0, 0)))
+    total = rows + sum(a.size // width for a in arrays)
+
+    def kernel(square_ref, *refs):
+        out = refs[-1]
+        for i in range(blocks):
+            out[:rows, i * 128 : (i + 1) * 128] = square_ref[i * rows : (i + 1) * rows, :]
+        first = rows
+        for ref in refs[:-1]:
+            size = ref.size // width if ref.ndim == 1 else ref.shape[0]
+            out[first : first + size, :] = ref[...].reshape(size, width)
+            first += size
+        if first < out.shape[0]:
+            out[first:, :] = jnp.zeros((out.shape[0] - first, width), SINGLE)
+
+    return pl.pallas_call(
+        kernel,
+        out_shape=jax.ShapeDtypeStruct((-(-total // 8) * 8, width), SINGLE),
+        name="pack_rows",
+    )(square, *arrays)
+
+
+def unpack_rows(packed, shapes, square):
+    width = packed.shape[1]
+    blocks = width // square[1]
+    rows = -(-square[0] // (8 * blocks)) * 8
+    whole = [packed[:rows, i * square[1] : (i + 1) * square[1]] for i in range(blocks)]
+    parts, first = [jnp.concatenate(whole, axis=0)[: square[0]]], rows
+    for size, _ in shapes:
+        parts.append(packed[first : first + size])
+        first += size
+    return parts
 
 
 def tree_sum(values):
@@ -212,8 +548,8 @@
         own, query, (((1,), (1,)), ((), ())), preferred_element_type=SINGLE
     )
     scores = jnp.where(key_ok, scores, MASKED)
-    expd = jnp.exp(scores - jnp.max(scores, axis=0, keepdims=True))
-    return expd / jnp.sum(expd, axis=0, keepdims=True)
+    expd = jnp.exp(scores - jnp.max(scores, axis=0))
+    return expd / jnp.sum(expd, axis=0)
 
 
 def over_rows(left, right):
@@ -277,7 +613,7 @@
                 (((1,), (1,)), ((), ())),
                 preferred_element_type=SINGLE,
             )
-            inner = jnp.sum(probs * grad_prob, axis=0, keepdims=True)
+            inner = jnp.sum(probs * grad_prob, axis=0)
             grad_score = (probs * (grad_prob - inner)).astype(HALF)
             grad_k = jnp.where(
                 own, jnp.dot(grad_score, query, preferred_element_type=SINGLE), grad_k
@@ -286,6 +622,66 @@
         out_ref[0, :, pl.ds(start, 128)] = (grad_q * scale).astype(HALF)
         out_ref[0, :, pl.ds(at_key, 128)] = grad_k.astype(HALF)
         out_ref[0, :, pl.ds(at_value, 128)] = grad_v.astype(HALF)
+
+
+def embed_kernel(chips, wide_ref, base_ref, gain_ref, offset_ref, *refs):
+    pieces, (start_ref, hat_ref, inv_ref, out_ref, whole_ref, staged, sems) = refs[:-7], refs[-7:]
+    copies, first = [], 0
+    for i, piece in enumerate(pieces):
+        size = piece.shape[0]
+        copies.append(
+            pltpu.make_async_copy(piece, staged.at[pl.ds(first, size)], sems.at[i])
+        )
+        first += size
+    for copy in copies:
+        copy.start()
+    for copy in copies:
+        copy.wait()
+    back = pltpu.make_async_copy(staged, whole_ref, sems.at[len(copies)])
+    back.start()
+    rows = wide_ref.shape[0] // chips
+
+    @pl.loop(0, chips)
+    def _(c):
+        at = pl.ds(pl.multiple_of(c * rows, rows), rows)
+        start = base_ref[at, :] + jnp.dot(
+            wide_ref[at, :], staged[...], preferred_element_type=SINGLE
+        )
+        result, normed, inv_std = norm_forward(start, gain_ref[...], offset_ref[...])
+        start_ref[at, :] = start
+        hat_ref[at, :] = normed
+        inv_ref[at, :] = inv_std
+        out_ref[at, :] = result.astype(HALF)
+
+    back.wait()
+
+
+def embed(chips, wide, base, gain, offset, pieces):
+    rows, width = base.shape
+    whole = pl.BlockSpec(memory_space=pltpu.VMEM)
+    return pl.pallas_call(
+        functools.partial(embed_kernel, chips),
+        out_shape=[
+            jax.ShapeDtypeStruct((rows, width), SINGLE),
+            jax.ShapeDtypeStruct((rows, width), SINGLE),
+            jax.ShapeDtypeStruct((rows, 1), SINGLE),
+            jax.ShapeDtypeStruct((rows, width), HALF),
+            jax.ShapeDtypeStruct((wide.shape[1], width), HALF),
+        ],
+        in_specs=[whole] * 4 + [pl.BlockSpec(memory_space=pl.ANY)] * len(pieces),
+        out_specs=[whole] * 4 + [pl.BlockSpec(memory_space=pl.ANY)],
+        scratch_shapes=[
+            pltpu.VMEM((wide.shape[1], width), HALF),
+            pltpu.SemaphoreType.DMA((len(pieces) + 1,)),
+        ],
+        compiler_params=pltpu.CompilerParams(vmem_limit_bytes=40 * 2**20),
+        cost_estimate=pl.CostEstimate(
+            flops=2 * rows * wide.shape[1] * width,
+            bytes_accessed=2 * wide.size + 2 * wide.shape[1] * width + 14 * base.size,
+            transcendentals=0,
+        ),
+        name="embed",
+    )(wide, base, gain[None], offset[None], *pieces)
 
 
 def attention_call(kernel, name, counts, arrays, out_width, flops):
@@ -332,7 +728,11 @@
         - jnp.mean(scaled, axis=-1, keepdims=True)
         - normed * jnp.mean(scaled * normed, axis=-1, keepdims=True)
     )
-    return (back, jnp.sum(upstream * normed, axis=0), jnp.sum(upstream, axis=0))
+    return (
+        back,
+        jnp.sum(upstream * normed, axis=0),
+        jnp.sum(upstream, axis=0),
+    )
 
 
 def gelu_parts(values):
@@ -387,6 +787,9 @@
     scale = (width // HEADS) ** (-0.5)
     me = lax.axis_index(AXES).astype(jnp.int32).reshape(1)
 
+    feed_layout = Layout([w_fc1, w_fc2], None)
+    feed = lax.all_gather(feed_layout.joined(), AXES, axis=0, tiled=False)
+
     code = wave_code(wavelengths).reshape(sensors * bands, -1)
     band_mask = (
         (jnp.arange(bands)[None, :] < band_count[:, None]).astype(SINGLE).reshape(-1, 1)
@@ -404,18 +807,11 @@
         .astype(HALF)
         .reshape(held * sensors * bands, per_row)
     )
-    generated = gather([kernel_own], me, count)[0]
-    generated = (
-        generated.reshape(spots // held, pieces, held * sensors * bands, per_row)
-        if pieces > 1
-        else generated
-    )
-    if pieces > 1:
-        generated = generated.transpose(0, 2, 1, 3)
-    generated = generated.reshape(spots * sensors * bands, width)
-
-    proj_qkv, proj_out = gather([w_qkv, w_out], me, count)
-    proj_down, proj_up = gather([w_fc2, w_fc1], me, count)
+    merged = pieces == 1 and w_qkv.shape[0] % 8 == 0
+    gather_kernel = Gather(Layout([kernel_own], None), me, count)
+    z_kernel = gather_kernel.along_z()
+    gather_attn = Gather(Layout([w_qkv, w_out], None), me, count)
+    gather_attn.data = after(gather_attn.data, gather_kernel.first)
 
     spot_of = jnp.pad(visible, ((0, 0), (lead, rows - length)), constant_values=-1)
     token = jnp.arange(rows)
@@ -430,6 +826,10 @@
         (row_ids // bands) % sensors,
         row_ids % bands,
     )
+    if merged:
+        order = sorted(range(count), key=lambda mask: position(mask, count))
+        block = jnp.asarray(order, jnp.int32)[row_spot // held]
+        row_spot = (block ^ me[0]) * held + row_spot % held
     source = jnp.where(
         row_sensor[None, :] == sensor_id[:, None], (row_band * spots + row_spot)[None, :], -1
     )
@@ -439,10 +839,10 @@
         .astype(HALF)
         .reshape(rows_all, -1)
     )
-    kern_chip = jnp.einsum(
-        "cvr,rd->cvd", spread, generated, preferred_element_type=SINGLE
-    ).astype(HALF)
-
+    gather_kernel.first_xy(patches_wide)
+    gather_attn.along_z()
+    gather_kernel.second_xy(*gather_attn.zs)
+    gather_attn.first_xy(gather_kernel.turn)
     side_len = jnp.where(chip_size == MAXP, SIDE, SIDE // 2).astype(jnp.int32)[:, None]
     quarter = width // 4
     freqs = 10000.0 ** (-jnp.arange(quarter, dtype=SINGLE) / quarter)
@@ -476,11 +876,39 @@
     grad_branch = grad_final.astype(HALF)
     g_fc2_bias = jnp.sum(grad_final, axis=0)
 
-    start = (
-        jnp.dot(patches_wide, generated, preferred_element_type=SINGLE) + base
-    )
-    normed_one, hat_one, inv_one = norm_forward(start, ln1_gain, ln1_bias)
-    normed_one = normed_one.astype(HALF)
+    gather_kernel.along_core(base, grad_branch)
+    own_pieces = [p for _, p in gather_kernel.pieces]
+    gather_attn.second_xy(*own_pieces[2:4])
+    if merged:
+        assert [m for ms, _ in gather_kernel.pieces for m in ms] == order
+        start, hat_one, inv_one, normed_one, generated = embed(
+            chips,
+            patches_wide,
+            after(base, gather_attn.turn),
+            ln1_gain,
+            ln1_bias,
+            [p.reshape(-1, width) for p in own_pieces],
+        )
+    else:
+        generated = gather_kernel.finish()[0].reshape(
+            spots // held, pieces, held * sensors * bands, per_row
+        )
+        generated = generated.transpose(0, 2, 1, 3).reshape(-1, width)
+        start = base + jnp.dot(patches_wide, generated, preferred_element_type=SINGLE)
+        normed_one, hat_one, inv_one = norm_forward(start, ln1_gain, ln1_bias)
+        normed_one = normed_one.astype(HALF)
+    proj_up, proj_down = place(
+        [after(feed, start)],
+        [list(range(count))],
+        (0, feed_layout.shape[0]),
+        feed_layout.splits,
+        feed_layout.shapes,
+        jnp.zeros_like(me),
+        count,
+    )
+    proj_up, proj_down = proj_up.reshape(width, -1), proj_down.reshape(-1, width)
+    gather_attn.along_core(proj_up)
+    proj_qkv, proj_out = gather_attn.finish()
     joined = jnp.dot(normed_one, proj_qkv, preferred_element_type=SINGLE).astype(HALF)
     joined = joined.reshape(chips, rows, -1)
     attn = attention_call(
@@ -502,9 +930,16 @@
     hidden = hidden_f.astype(HALF)
     grad_up = (grad_hidden * hidden_slope).astype(HALF)
 
-    g_down = jnp.einsum("rf,rd->fd", hidden, grad_branch, preferred_element_type=SINGLE)
-    g_up = jnp.einsum("rd,rf->df", normed_two, grad_up, preferred_element_type=SINGLE)
-    g_down, g_up = scatter([g_down.astype(HALF), g_up.astype(HALF)], me, count)
+    g_down = jnp.einsum(
+        "rf,rd->fd", hidden, grad_branch, preferred_element_type=SINGLE
+    ).astype(HALF)
+    g_up = jnp.einsum(
+        "rd,rf->df", normed_two, grad_up, preferred_element_type=SINGLE
+    ).astype(HALF)
+    grad_up, g_up, g_down = lax.optimization_barrier((grad_up, g_up, g_down))
+    scatter_up = Scatter(count, me).along_core(g_up)
+    g_down = lax.psum_scatter(g_down, AXES, scatter_dimension=0, tiled=True)
+    grad_up = after(grad_up, *scatter_up.sent)
     g_fc1_bias = jnp.sum(grad_up.astype(SINGLE), axis=0)
     grad_norm_two = jnp.einsum(
         "rf,df->rd", grad_up, proj_up, preferred_element_type=SINGLE
@@ -515,12 +950,16 @@
     grad_middle = grad_final + back_two
     grad_attn_out = grad_middle.astype(HALF)
     g_out_bias = jnp.sum(grad_attn_out.astype(SINGLE), axis=0)
-    g_out = jnp.einsum("rd,re->de", attn, grad_attn_out, preferred_element_type=SINGLE)
+    g_out = jnp.einsum(
+        "rd,re->de", attn, grad_attn_out, preferred_element_type=SINGLE
+    ).astype(HALF)
     grad_attn = (
         jnp.einsum("re,de->rd", grad_attn_out, proj_out, preferred_element_type=SINGLE)
         .astype(HALF)
         .reshape(chips, rows, width)
     )
+    scatter_up.first_xy(grad_attn)
+    grad_attn = after(grad_attn, *scatter_up.sent)
     grad_joined = attention_call(
         functools.partial(attend_back_kernel, width, scale),
         "attend_back",
@@ -529,13 +968,21 @@
         3 * width,
         10 * chips * rows * rows * width,
     ).reshape(rows_all, -1)
+    scatter_up.second_xy(grad_joined)
     g_qkv = jnp.einsum(
-        "rd,re->de", normed_one, grad_joined, preferred_element_type=SINGLE
-    )
-    g_qkv, g_out = scatter([g_qkv.astype(HALF), g_out.astype(HALF)], me, count)
+        "rd,re->de",
+        normed_one,
+        after(grad_joined, *scatter_up.sent),
+        preferred_element_type=SINGLE,
+    ).astype(HALF)
+    scatter_attn = Scatter(count, me).along_core(g_qkv)
     grad_norm_one = jnp.einsum(
-        "re,de->rd", grad_joined, proj_qkv, preferred_element_type=SINGLE
-    )
+        "re,de->rd",
+        after(grad_joined, *scatter_attn.sent),
+        proj_qkv,
+        preferred_element_type=SINGLE,
+    )
+    scatter_attn.along_core(g_out)
     back_one, g_ln1_gain, g_ln1_bias = norm_backward(
         grad_norm_one, hat_one, inv_one, ln1_gain
     )
@@ -545,14 +992,60 @@
         .astype(HALF)
         .reshape(rows_all, width)
     )
-    kern_terms = jnp.einsum(
-        "rk,rd->kd", patches_wide, grad_embedded, preferred_element_type=SINGLE
+    scatter_up.across_z(grad_embedded)
+    scatter_attn.first_xy(grad_embedded)
+    grad_late = after(grad_embedded, *scatter_up.sent, *scatter_attn.sent)
+    scatter_kernel = Scatter(count, me, relative=merged)
+
+    def kernel_terms(wide):
+        return jnp.einsum(
+            "rk,rd->kd", wide, grad_late, preferred_element_type=SINGLE
+        ).astype(HALF)
+
+    if merged:
+        half = patches_wide.shape[1] // 2
+        far = kernel_terms(patches_wide[:, half:]).reshape(count // 2, -1, width)
+        kern_terms = kernel_terms(after(patches_wide, far)[:, :half])
+        scatter_kernel.with_core(kern_terms.reshape(count // 2, -1, width), far)
+    else:
+        kern_terms = kernel_terms(patches_wide)
+        if pieces > 1:
+            kern_terms = kern_terms.reshape(
+                spots // held, held * sensors * bands, pieces, per_row
+            ).transpose(0, 2, 1, 3)
+        scatter_kernel.along_core(kern_terms.reshape(-1, per_row))
+    scatter_up.across_rest(kern_terms)
+    scatter_kernel.first_xy(*scatter_up.sent)
+    kern_chip = jnp.einsum(
+        "cvr,rd->cvd",
+        spread,
+        after(generated, *scatter_kernel.sent),
+        preferred_element_type=SINGLE,
     ).astype(HALF)
-    if pieces > 1:
-        kern_terms = kern_terms.reshape(
-            spots // held, held * sensors * bands, pieces, per_row
-        ).transpose(0, 2, 1, 3)
-    grad_kernel = scatter([kern_terms.reshape(-1, per_row)], me, count)[0]
+    scatter_attn.second_xy(kern_chip)
+    scatter_kernel.second_xy(*scatter_attn.sent)
+    final = middle + jnp.dot(
+        after(hidden, *scatter_kernel.sent), proj_down, preferred_element_type=SINGLE
+    )
+    mixed = ((final + fc2_bias) * keep_rows).astype(HALF)
+    mixed = mixed.reshape(chips, rows, width)[:, :length]
+    scatter_attn.across_z(mixed)
+    scatter_kernel.across_z(*scatter_attn.sent)
+    scattered = jnp.einsum(
+        "ctp,ctd->cpd",
+        chosen,
+        after(grad_embedded, *scatter_kernel.sent).reshape(chips, rows, width),
+        preferred_element_type=SINGLE,
+    ).astype(HALF)
+    scatter_kernel.across_rest(scattered)
+    scatter_attn.across_rest(*scatter_kernel.sent)
+    g_pixels = jnp.einsum(
+        "cpd,cvd->cpv",
+        after(scattered, *scatter_attn.sent),
+        kern_chip,
+        preferred_element_type=SINGLE,
+    )
+    grad_kernel = scatter_kernel.finish(g_pixels)[0]
     grad_kernel = grad_kernel.reshape(held, sensors * bands, per_row)
     grad_embed = split_dot("prc,pch->rh", grad_kernel, wave2_own)
     g_wave2 = split_dot("prc,rh->pch", grad_kernel, embed_low).reshape(columns, -1)
@@ -563,69 +1056,56 @@
     g_time_place = jnp.einsum(
         "cd,md->cm", grad_meta, w_meta.astype(SINGLE), precision=PRECISE
     )
-    g_patch_bias = jnp.sum(by_chip * is_patch, axis=(0, 1))
-    meta_rows = time_place.shape[1]
-    small = total_over(
-        jnp.concatenate(
-            [
-                g_w_meta,
-                g_fc1_bias.reshape(-1, width),
-                g_cls[None],
-                g_patch_bias[None],
-                g_ln1_gain[None],
-                g_ln1_bias[None],
-                g_out_bias[None],
-                g_ln2_gain[None],
-                g_ln2_bias[None],
-                g_fc2_bias[None],
-                jnp.pad(grad_embed.reshape(-1), (0, -grad_embed.size % width)).reshape(
-                    -1, width
-                ),
-            ],
-            axis=0,
-        ),
-        count,
-    )
-    base_row = meta_rows + fc1_bias.shape[0] // width
-    grad_embed = small[base_row + 8 :].reshape(-1)[: grad_embed.size]
-    grad_embed = grad_embed.reshape(sensors * bands, -1)
+    g_patch_bias = jnp.sum(
+        (by_chip * is_patch).reshape(rows_all, width), axis=0, keepdims=True
+    )
+    ups = fc1_bias.shape[0] // width
+    shapes = [(time_place.shape[1], width), (ups, width)] + [(1, width)] * 8
+    packed = pack_rows(
+        [
+            g_w_meta,
+            *[g_fc1_bias[i * width : (i + 1) * width] for i in range(ups)],
+            g_cls,
+            g_patch_bias,
+            g_ln1_gain,
+            g_ln1_bias,
+            g_out_bias,
+            g_ln2_gain,
+            g_ln2_bias,
+            g_fc2_bias,
+        ],
+        grad_embed,
+        width,
+    )
+    g_down = after(g_down, packed).astype(SINGLE)
+    g_up = scatter_up.finish(packed)[0]
+    g_qkv, g_out = scatter_attn.finish(packed)
+    packed = total_over(packed, count)
+    grad_embed, *small = unpack_rows(packed, shapes, grad_embed.shape)
     grad_pre = grad_embed * band_mask * activ_slope
     g_wave1 = jnp.einsum("rh,rk->hk", code, grad_pre, precision=PRECISE)
     g_wave1_bias = jnp.sum(grad_pre, axis=0)
-
-
-    scattered = jnp.einsum(
-        "ctp,ctd->cpd",
-        chosen,
-        grad_embedded.reshape(chips, rows, width),
-        preferred_element_type=SINGLE,
-    ).astype(HALF)
-    g_pixels = jnp.einsum(
-        "cpd,cvd->cpv", scattered, kern_chip, preferred_element_type=SINGLE
-    )
-    final = middle + jnp.dot(hidden, proj_down, preferred_element_type=SINGLE) + fc2_bias
-    mixed = (final * keep_rows).astype(HALF).reshape(chips, rows, width)[:, :length]
     return (
         mixed,
         g_pixels,
         g_time_place,
-        small[base_row],
-        small[:meta_rows],
+        small[2].reshape(-1),
+        small[0],
         g_wave1,
         g_wave1_bias,
         g_wave2,
-        small[base_row + 1],
-        small[base_row + 2],
-        small[base_row + 3],
+        small[3].reshape(-1),
+        small[4].reshape(-1),
+        small[5].reshape(-1),
         g_qkv,
         g_out,
-        small[base_row + 4],
-        small[base_row + 5],
-        small[base_row + 6],
+        small[6].reshape(-1),
+        small[7].reshape(-1),
+        small[8].reshape(-1),
         g_up,
-        small[meta_rows:base_row].reshape(-1),
+        small[1].reshape(-1),
         g_down,
-        small[base_row + 7],
+        small[9].reshape(-1),
     )
 
 

time: 492 us -> 418 us (0.85)
  waiting for transfers between devices: 167 us -> 73.2 us
  Pallas kernels: 49.4 us -> 88.9 us
  other arithmetic: 59.7 us -> 31.1 us
  between operations: 2.78 us -> 15.7 us
  local copies, waits for them, and re-layouts: 49.4 us -> 56 us
  starting transfers between devices: 61.8 us -> 55.2 us
    ppermute x58 -> x49, waiting for transfers between devices: 167 us -> 72.7 us  [swap(): return lax.ppermute(values, AXES, [(i, i ^ mask) for i in range(count)])]
    pallas_call x3 -> x23, Pallas kernels: 19.3 us -> 58.4 us  [the longest x15 30.6 us: added(): pl.pallas_call(functools.partial(add_kernel, outs_of), out_shape=out_shap...]
    unnamed x191 -> x200, local copies, waits for them, and re-layouts: 28.2 us -> 46.9 us
    unnamed x26 -> x3, other arithmetic: 14.8 us -> 0.01 us
    dot_general x7 -> x8, matrix products: 45.1 us -> 34.4 us  [the longest x1 9.9 us: local(): jnp.einsum('cvr,rd->cvd', spread, after(generated, *scatter_kernel.sent),...]
    concatenate x14 -> x1, other arithmetic: 11.3 us -> 0.78 us  [joined(): jnp.concatenate([self.shards[which][row:row + size] for which, row, size,...]
    add x8 -> x1, other arithmetic: 8.72 us -> 0.07 us  [local(): row_band * spots + row_spot]
    ppermute x58 -> x49, starting transfers between devices: 61.8 us -> 55.1 us  [swap(): return lax.ppermute(values, AXES, [(i, i ^ mask) for i in range(count)])]
  transfers between devices with their start and end apart: 58 -> 51, of which waited for: 22 -> 14; matrix products, arithmetic and copies ran while one was open for 26% -> 23% of each run, Pallas kernels for 5% -> 16%
where the time goes in v2:
time: 418 us; the launch traced here: 410 us
  matrix products  90.3 us (22%)
  Pallas kernels  88.9 us (21%)
  waiting for transfers between devices  73.2 us (18%)
  local copies, waits for them, and re-layouts  56 us (13%)
  starting transfers between devices  55.2 us (13%)
  other arithmetic  31.1 us (7%)
  between operations  15.7 us (4%)
    ppermute x49, waiting for transfers between devices, swap(): return lax.ppermute(values, AXES, [(i, i ^ mask) for i in range(count)])  72.7 us
    ppermute x49, starting transfers between devices, swap(): return lax.ppermute(values, AXES, [(i, i ^ mask) for i in range(count)])  55.1 us
    unnamed x200, local copies, waits for them, and re-layouts  46.9 us
    pallas_call x15, Pallas kernels, added(): pl.pallas_call(functools.partial(add_kernel, outs_of), out_shape=out_shap...  30.6 us
    pallas_call x2, Pallas kernels, attention_call(): pl.pallas_call(kernel, out_shape=jax.ShapeDtypeStruct((chips, rows, out_w...  30.5 us
    pallas_call x2, Pallas kernels, place(): pl.pallas_call(functools.partial(place_kernel, masks, part, splits), out_...  10.1 us
    dot_general x1, matrix products, local(): jnp.einsum('cvr,rd->cvd', spread, after(generated, *scatter_kernel.sent),...  9.9 us
    dot_general x2, matrix products, kernel_terms(): jnp.einsum('rk,rd->kd', wide, grad_late, preferred_element_type=SINGLE)  8.9 us
  transfers between devices with their start and end apart: 51, of which 14 were waited for; matrix products, arithmetic and copies ran while one was open for 23% of the time, Pallas kernels for 16%

profile of v2, /device:TPU:0, one launch (start us, length us, event | category | flops | bytes accessed | tf_op | source)
XLA Modules:
  0.0 410.4 jit_solution(8267519625353352836)
XLA Ops:
  22.9 4.0 collective-permute-start
  39.5 8.2 %fusion.10 = bf16[2,272,3328]{2,1,0:T(8,128)(2,1)} fusion(s32[2,3328]{1,0:T(2,128)} %compare_select_fusion.7, bf16[2,1024,832]{1,2,0:T(8,128)(2,1)S(1)} %copy-done, s32[2,272]{1,0:T(2,128)S(1)} %copy-done.81), kind=kOutput, calls=%fused_computation.15 | convolution fusion | flops 3947857920 | bytes 7057536 | tf_op jit(solution)/shard_map/ctv,cvr->ctr/dot_general | solution.py:838
  54.0 13.7 %collective-permute-done.3.refs_2_ = bf16[2,104,768]{2,1,0:T(8,128)(2,1)S(1)} collective-permute-done((bf16[2,104,768]{2,1,0:T(8,128)(2,1)}, bf16[2,104,768]{2,1,0:T(8,128)(2,1)S(1)}, u32[]{:S(2)}, u32[]{:S(2)}) %collective-permute-start.3) | collective-permute-done | bytes 319520 | tf_op jit(solution)/shard_map/ppermute | solution.py:43
  72.1 7.3 %collective-permute-done.1.refs_1_ = bf16[1,24,3072]{2,1,0:T(8,128)(2,1)S(1)} collective-permute-done((bf16[1,24,3072]{2,1,0:T(8,128)(2,1)S(1)}, bf16[1,24,3072]{2,1,0:T(8,128)(2,1)S(1)}, u32[]{:S(2)}, u32[]{:S(2)}) %collective-permute-start.1) | collective-permute-done | bytes 147488 | tf_op jit(solution)/shard_map/ppermute | solution.py:43
  90.7 4.4 %collective-permute-start.8 = (bf16[2,24,3072]{2,1,0:T(8,128)(2,1)S(1)}, bf16[2,24,3072]{2,1,0:T(8,128)(2,1)S(1)}, u32[]{:S(2)}, u32[]{:S(2)}) collective-permute-start(bf16[2,24,3072]{2,1,0:T(8,128)(2,1)S(1)} %copy-done.50), channel_id=1, source_target_pairs={{0,8},{1,9},{2,10},{3,11},{4,12},{5,13},{6,14},{7,15},{8,0},{9,1},... | collective-permute-start | bytes 884744 | tf_op jit(solution)/shard_map/ppermute | solution.py:43
  96.9 13.6 %collective-permute-done.7 = bf16[4,104,768]{2,1,0:T(8,128)(2,1)} collective-permute-done((bf16[4,104,768]{2,1,0:T(8,128)(2,1)}, bf16[4,104,768]{2,1,0:T(8,128)(2,1)}, u32[]{:S(2)}, u32[]{:S(2)}) %collective-permute-start.7) | collective-permute-done | bytes 639008 | tf_op jit(solution)/shard_map/ppermute | solution.py:43
  111.0 3.5 collective-permute-done.5.refs_1_
  116.7 6.6 %collective-permute-done.9.refs_3_ = bf16[2,24,3072]{2,1,0:T(8,128)(2,1)S(1)} collective-permute-done((bf16[2,24,3072]{2,1,0:T(8,128)(2,1)S(1)}, bf16[2,24,3072]{2,1,0:T(8,128)(2,1)S(1)}, u32[]{:S(2)}, u32[]{:S(2)}) %collective-permute-start.9) | collective-permute-done | bytes 294944 | tf_op jit(solution)/shard_map/ppermute | solution.py:43
  129.5 8.2 %embed.1 = (f32[544,768]{1,0:T(8,128)S(1)}, f32[544,768]{1,0:T(8,128)S(1)}, f32[544,1]{1,0:T(8,128)S(1)}, bf16[544,768]{1,0:T(8,128)(2,1)S(1)}, bf16[3328,768]{1,0:T(8,128)(2,1)}) custom-call(bf16[544,3328]{1,0:T(8,128)(2,1)} %bitcast.178, f32[544,768]{1,0:T(8,128)S(1)} %fusion.19.base_ref, f32[1,768]{1,0:T(1,128)S(1)} %broadcast_in_dim.139.gain_ref, ...), custom_call_target="tpu_custom_call" | custom-call | flops 2780823552 | bytes 14581760 | tf_op jit(solution)/shard_map/embed/pallas_call | solution.py:662
  141.6 3.7 copy-done.2
  145.3 6.5 %place.2 = (bf16[32,24,3072]{2,1,0:T(8,128)(2,1)S(1)}, bf16[32,4,24,768]{3,2,1,0:T(8,128)(2,1)S(1)}) custom-call(s32[1]{0:T(128)} %constant.146.clone.1.index_ref, bf16[32,24,6144]{2,1,0:T(8,128)(2,1)S(1)} %bitcast.124), custom_call_target="tpu_custom_call" | custom-call | bytes 18874368 | tf_op jit(solution)/shard_map/place/pallas_call | solution.py:111
  158.4 3.6 place.3
  164.2 13.3 %attend.1 = bf16[2,272,768]{2,1,0:T(8,128)(2,1)S(1)} custom-call(s32[2]{0:T(128)S(1)} %get-tuple-element.209.count_ref, bf16[2,272,2304]{2,1,0:T(8,128)(2,1)S(1)} %bitcast.125), custom_call_target="tpu_custom_call" | custom-call | flops 454557696 | bytes 10485760 | tf_op jit(solution)/shard_map/attend/pallas_call | solution.py:693
  180.6 5.7 %multiply_convert_fusion = (bf16[544,3072]{1,0:T(8,128)(2,1)S(1)}, f32[544,3072]{1,0:T(8,128)}) fusion(f32[3072]{0:T(1024)S(1)} %copy-done.85, bf16[768,3072]{1,0:T(8,128)(2,1)S(1)} %bitcast.139, f32[544,768]{1,0:T(8,128)S(1)} %get-tuple-element.214, f32[768]{0:T(1024)S(1)} %copy-done.87, f32[768]{0:T(1024)S(1)} %copy-done.80, f32[544]{0:T(1024)S(1)} %add_rsqrt_fusion, ...), kind=kOutput, calls=%fused_computation.13 | convolution fusion | flops 2579030016 | bytes 16439552 | tf_op jit(solution)/shard_map/dot_general | solution.py:928
  188.0 5.6 %convolution_convert_fusion.1 = bf16[3072,768]{1,0:T(8,128)(2,1)} fusion(bf16[544,3072]{1,0:T(8,128)(2,1)S(1)} %get-tuple-element.154, bf16[544,768]{1,0:T(8,128)(2,1)S(1)} %copy-done.51), kind=kOutput, calls=%fused_computation.18 | convolution fusion | flops 2569273344 | bytes 8896512 | tf_op jit(solution)/shard_map/rf,rd->fd/dot_general | solution.py:933
  193.7 7.3 %fusion.9 = bf16[544,3072]{1,0:T(8,128)(2,1)S(1)} fusion(f32[544,3072]{1,0:T(8,128)} %get-tuple-element.216, bf16[544,768]{1,0:T(8,128)(2,1)S(1)} %bitcast.189, bf16[3072,768]{1,0:T(8,128)(2,1)} %bitcast.132, f32[3072]{0:T(1024)S(1)} %copy-done.85), kind=kOutput, calls=%fused_computation.11 | convolution fusion | flops 2585296896 | bytes 15593472 | tf_op jit(solution)/shard_map/rd,fd->rf/dot_general | solution.py:925
  201.0 4.8 %convolution_convert_fusion.2 = bf16[768,3072]{1,0:T(8,128)(2,1)S(1)} fusion(bf16[544,3072]{1,0:T(8,128)(2,1)S(1)} %fusion.9, f32[544,768]{1,0:T(8,128)S(1)} %copy-done.36, f32[768]{0:T(1024)S(1)} %copy-done.87, f32[768]{0:T(1024)S(1)} %copy-done.80, f32[544]{0:T(1024)S(1)} %add_rsqrt_fusion, f32[544]{0:T(1024)S(1)} %broadcast_multiply_fusion.5), kind=kOutput, calls=%fused_computation.19 | convolution fusion | flops 2571362304 | bytes 9742592 | tf_op jit(solution)/shard_map/rd,rf->df/dot_general | solution.py:936
  208.5 6.2 %multiply_reduce_fusion = (f32[768]{0:T(1024)}, f32[544]{0:T(1024)S(1)}, f32[544]{0:T(1024)S(1)}, f32[768]{0:T(1024)}, f32[544,768]{1,0:T(8,128)S(1)}) fusion(f32[544,768]{1,0:T(8,128)S(1)} %copy-done.36, f32[544]{0:T(1024)S(1)} %add_rsqrt_fusion, f32[544]{0:T(1024)S(1)} %broadcast_multiply_fusion.5, f32[768]{0:T(1024)S(1)} %copy-done.80, ...), kind=kOutput, calls=%fused_computation.33 | convolution fusion | flops 2570671616 | bytes 11421184 | tf_op jit(solution)/shard_map/rf,df->rd/dot_general | solution.py:944
  218.6 3.7 add_xy.3
  228.7 17.3 %attend_back.1 = bf16[2,272,2304]{2,1,0:T(8,128)(2,1)S(1)} custom-call(s32[2]{0:T(128)S(1)} %get-tuple-element.209.count_ref, bf16[2,272,2304]{2,1,0:T(8,128)(2,1)S(1)} %bitcast.126, bf16[2,272,768]{2,1,0:T(8,128)(2,1)S(1)} %bitcast.129), custom_call_target="tpu_custom_call" | custom-call | flops 1136394240 | bytes 10485760 | tf_op jit(solution)/shard_map/attend_back/pallas_call | solution.py:693
  249.6 3.2 convolution_convert_fusion
  263.7 3.2 add_xy.4
  266.9 3.7 convolution_convert_fusion.5
  280.6 5.2 %convolution_convert_fusion.4 = bf16[1664,768]{1,0:T(8,128)(2,1)} fusion(bf16[544,768]{1,0:T(8,128)(2,1)S(1)} %multiply_convert_fusion.2, bf16[544,3328]{1,0:T(8,128)(2,1)} %bitcast.179), kind=kOutput, calls=%fused_computation.21 | convolution fusion | flops 1391689728 | bytes 5201920 | tf_op jit(solution)/shard_map/rk,rd->kd/dot_general | solution.py:1001
  289.1 3.2 add_xy.5
  294.4 9.9 %fusion.13 = bf16[2,832,768]{2,1,0:T(8,128)(2,1)S(1)} fusion(bf16[3328,768]{1,0:T(8,128)(2,1)S(1)} %bitcast.199, s32[2,3328]{1,0:T(2,128)S(1)} %copy-done.73), kind=kOutput, calls=%fused_computation.26 | convolution fusion | flops 8512864256 | bytes 7694336 | tf_op jit(solution)/shard_map/cvr,rd->cvd/dot_general | solution.py:1019
  324.4 3.5 collective-permute-done.33.refs_3_
  332.3 14.6 %collective-permute-done.38.refs_4_ = bf16[2,104,768]{2,1,0:T(8,128)(2,1)S(1)} collective-permute-done((bf16[2,104,768]{2,1,0:T(8,128)(2,1)S(1)}, bf16[2,104,768]{2,1,0:T(8,128)(2,1)S(1)}, u32[]{:S(2)}, u32[]{:S(2)}) %collective-permute-start.38) | collective-permute-done | bytes 319520 | tf_op jit(solution)/shard_map/ppermute | solution.py:43
  354.9 4.8 %fusion.86 = f32[2,1024,832]{1,2,0:T(8,128)} fusion(bf16[2,1024,768]{2,1,0:T(8,128)(2,1)S(1)} %convolution_convert_fusion.6, bf16[2,832,768]{2,1,0:T(8,128)(2,1)S(1)} %fusion.13), kind=kOutput, calls=%fused_computation.237 | convolution fusion | flops 2617245696 | bytes 12517376 | tf_op jit(solution)/shard_map/cpd,cvd->cpv/dot_general | solution.py:1042
  370.3 4.3 %collective-permute-start.43 = (f32[40,768]{1,0:T(8,128)S(1)}, f32[40,768]{1,0:T(8,128)S(1)}, u32[]{:S(2)}, u32[]{:S(2)}) collective-permute-start(f32[40,768]{1,0:T(8,128)S(1)} %add.265), channel_id=1, source_target_pairs={{0,5},{1,4},{2,7},{3,6},{4,1},{5,0},{6,3},{7,2},{8,13},{9,12},{10,... | collective-permute-start | bytes 368648 | tf_op jit(solution)/shard_map/ppermute | solution.py:43
  375.6 4.2 %collective-permute-done.43 = f32[40,768]{1,0:T(8,128)S(1)} collective-permute-done((f32[40,768]{1,0:T(8,128)S(1)}, f32[40,768]{1,0:T(8,128)S(1)}, u32[]{:S(2)}, u32[]{:S(2)}) %collective-permute-start.43) | collective-permute-done | bytes 122912 | tf_op jit(solution)/shard_map/ppermute | solution.py:43
  381.8 3.7 collective-permute-start.46
  (420 shorter events, 183.9 us)
Async XLA Ops:
  7.2 134.4 %all-gather.3.cloned.1.call-start = ((), (), s32[]{:S(2)}) async-start(), calls=%async_computation.2 | async-start | bytes 9732096 | tf_op jit(solution)/shard_map/all_gather | solution.py:791
  14.6 378.9 %reduce-scatter.2.cloned.1.call-start = ((), (), s32[]{:S(2)}) async-start(), calls=%async_computation.1 | async-start | bytes 4866048 | tf_op jit(solution)/shard_map/reduce_scatter | solution.py:941
  22.9 25.0 %collective-permute-start = (bf16[1,104,768]{2,1,0:T(8,128)(2,1)}, bf16[1,104,768]{2,1,0:T(8,128)(2,1)}, u32[]{:S(2)}, u32[]{:S(2)}) collective-permute-start(bf16[1,104,768]{2,1,0:T(8,128)(2,1)} %bitcast.192), channel_id=1, source_target_pairs={{0,16},{1,17},{2,18},{3,19},{4,20},{5,21},{6,22},{7,23},{8,24},{9,... | collective-permute-start | bytes 479240 | tf_op jit(solution)/shard_map/ppermute | solution.py:43
  49.9 17.9 %collective-permute-start.3 = (bf16[2,104,768]{2,1,0:T(8,128)(2,1)}, bf16[2,104,768]{2,1,0:T(8,128)(2,1)S(1)}, u32[]{:S(2)}, u32[]{:S(2)}) collective-permute-start(bf16[2,104,768]{2,1,0:T(8,128)(2,1)} %stack.4.refs_0_), channel_id=1, source_target_pairs={{0,8},{1,9},{2,10},{3,11},{4,12},{5,13},{6,14},{7,15},{8,0},{9,1},... | collective-permute-start | bytes 958472 | tf_op jit(solution)/shard_map/ppermute | solution.py:43
  52.4 29.3 %collective-permute-start.2 = (bf16[2,104,768]{2,1,0:T(8,128)(2,1)}, bf16[2,104,768]{2,1,0:T(8,128)(2,1)S(1)}, u32[]{:S(2)}, u32[]{:S(2)}) collective-permute-start(bf16[2,104,768]{2,1,0:T(8,128)(2,1)} %stack.4.refs_0_), channel_id=1, source_target_pairs={{0,1},{1,0},{2,3},{3,2},{4,5},{5,4},{6,7},{7,6},{8,9},{9,8},{10,11... | collective-permute-start | bytes 958472 | tf_op jit(solution)/shard_map/ppermute | solution.py:43
  67.7 14.0 %collective-permute-start.4 = (bf16[2,104,768]{2,1,0:T(8,128)(2,1)S(1)}, bf16[2,104,768]{2,1,0:T(8,128)(2,1)S(1)}, u32[]{:S(2)}, u32[]{:S(2)}) collective-permute-start(bf16[2,104,768]{2,1,0:T(8,128)(2,1)S(1)} %collective-permute-done.3.refs_2_), channel_id=1, source_target_pairs={{0,4},{1,5},{2,6},{3,7},{4,0},{5,1},{6,2},{7,3},{8,12},{9,13},{10,... | collective-permute-start | bytes 958472 | tf_op jit(solution)/shard_map/ppermute | solution.py:43
  85.4 25.1 %collective-permute-start.7 = (bf16[4,104,768]{2,1,0:T(8,128)(2,1)}, bf16[4,104,768]{2,1,0:T(8,128)(2,1)}, u32[]{:S(2)}, u32[]{:S(2)}) collective-permute-start(bf16[4,104,768]{2,1,0:T(8,128)(2,1)} %get-tuple-element.106), channel_id=1, source_target_pairs={{0,1},{1,0},{2,3},{3,2},{4,5},{5,4},{6,7},{7,6},{8,9},{9,8},{10,11... | collective-permute-start | bytes 1916936 | tf_op jit(solution)/shard_map/ppermute | solution.py:43
  86.9 23.6 %collective-permute-start.6 = (bf16[4,104,768]{2,1,0:T(8,128)(2,1)}, bf16[4,104,768]{2,1,0:T(8,128)(2,1)}, u32[]{:S(2)}, u32[]{:S(2)}) collective-permute-start(bf16[4,104,768]{2,1,0:T(8,128)(2,1)} %get-tuple-element.105), channel_id=1, source_target_pairs={{0,4},{1,5},{2,6},{3,7},{4,0},{5,1},{6,2},{7,3},{8,12},{9,13},{10,... | collective-permute-start | bytes 1916936 | tf_op jit(solution)/shard_map/ppermute | solution.py:43
  90.7 35.7 %collective-permute-start.10 = (bf16[4,104,768]{2,1,0:T(8,128)(2,1)S(1)}, bf16[4,104,768]{2,1,0:T(8,128)(2,1)}, u32[]{:S(2)}, u32[]{:S(2)}) collective-permute-start(bf16[4,104,768]{2,1,0:T(8,128)(2,1)S(1)} %copy-done.5), channel_id=1, source_target_pairs={{0,2},{1,3},{2,0},{3,1},{4,6},{5,7},{6,4},{7,5},{8,10},{9,11},{10,... | collective-permute-start | bytes 1916936 | tf_op jit(solution)/shard_map/ppermute | solution.py:43
  90.7 20.3 %collective-permute-start.8 = (bf16[2,24,3072]{2,1,0:T(8,128)(2,1)S(1)}, bf16[2,24,3072]{2,1,0:T(8,128)(2,1)S(1)}, u32[]{:S(2)}, u32[]{:S(2)}) collective-permute-start(bf16[2,24,3072]{2,1,0:T(8,128)(2,1)S(1)} %copy-done.50), channel_id=1, source_target_pairs={{0,8},{1,9},{2,10},{3,11},{4,12},{5,13},{6,14},{7,15},{8,0},{9,1},... | collective-permute-start | bytes 884744 | tf_op jit(solution)/shard_map/ppermute | solution.py:43
  95.0 19.5 %collective-permute-start.5 = (bf16[2,24,3072]{2,1,0:T(8,128)(2,1)S(1)}, bf16[2,24,3072]{2,1,0:T(8,128)(2,1)S(1)}, u32[]{:S(2)}, u32[]{:S(2)}) collective-permute-start(bf16[2,24,3072]{2,1,0:T(8,128)(2,1)S(1)} %copy-done.50), channel_id=1, source_target_pairs={{0,1},{1,0},{2,3},{3,2},{4,5},{5,4},{6,7},{7,6},{8,9},{9,8},{10,11... | collective-permute-start | bytes 884744 | tf_op jit(solution)/shard_map/ppermute | solution.py:43
  110.4 19.0 %collective-permute-start.11 = (bf16[4,104,768]{2,1,0:T(8,128)(2,1)S(1)}, bf16[4,104,768]{2,1,0:T(8,128)(2,1)}, u32[]{:S(2)}, u32[]{:S(2)}) collective-permute-start(bf16[4,104,768]{2,1,0:T(8,128)(2,1)S(1)} %copy-done.6), channel_id=1, source_target_pairs={{0,2},{1,3},{2,0},{3,1},{4,6},{5,7},{6,4},{7,5},{8,10},{9,11},{10,... | collective-permute-start | bytes 1916936 | tf_op jit(solution)/shard_map/ppermute | solution.py:43
  110.5 19.0 %collective-permute-start.13 = (bf16[4,104,768]{2,1,0:T(8,128)(2,1)}, bf16[4,104,768]{2,1,0:T(8,128)(2,1)}, u32[]{:S(2)}, u32[]{:S(2)}) collective-permute-start(bf16[4,104,768]{2,1,0:T(8,128)(2,1)} %collective-permute-done.7), channel_id=1, source_target_pairs={{0,2},{1,3},{2,0},{3,1},{4,6},{5,7},{6,4},{7,5},{8,10},{9,11},{10,... | collective-permute-start | bytes 1916936 | tf_op jit(solution)/shard_map/ppermute | solution.py:43
  111.0 18.5 %collective-permute-start.12 = (bf16[4,104,768]{2,1,0:T(8,128)(2,1)}, bf16[4,104,768]{2,1,0:T(8,128)(2,1)}, u32[]{:S(2)}, u32[]{:S(2)}) collective-permute-start(bf16[4,104,768]{2,1,0:T(8,128)(2,1)} %collective-permute-done.6), channel_id=1, source_target_pairs={{0,2},{1,3},{2,0},{3,1},{4,6},{5,7},{6,4},{7,5},{8,10},{9,11},{10,... | collective-permute-start | bytes 1916936 | tf_op jit(solution)/shard_map/ppermute | solution.py:43
  126.2 25.6 %collective-permute-start.15 = (bf16[4,24,3072]{2,1,0:T(8,128)(2,1)}, bf16[4,24,3072]{2,1,0:T(8,128)(2,1)S(1)}, u32[]{:S(2)}, u32[]{:S(2)}) collective-permute-start(bf16[4,24,3072]{2,1,0:T(8,128)(2,1)} %get-tuple-element.115.refs_1_), channel_id=1, source_target_pairs={{0,1},{1,0},{2,3},{3,2},{4,5},{5,4},{6,7},{7,6},{8,9},{9,8},{10,11... | collective-permute-start | bytes 1769480 | tf_op jit(solution)/shard_map/ppermute | solution.py:43
  126.4 25.4 %collective-permute-start.14 = (bf16[4,24,3072]{2,1,0:T(8,128)(2,1)}, bf16[4,24,3072]{2,1,0:T(8,128)(2,1)}, u32[]{:S(2)}, u32[]{:S(2)}) collective-permute-start(bf16[4,24,3072]{2,1,0:T(8,128)(2,1)} %get-tuple-element.114.refs_0_), channel_id=1, source_target_pairs={{0,4},{1,5},{2,6},{3,7},{4,0},{5,1},{6,2},{7,3},{8,12},{9,13},{10,... | collective-permute-start | bytes 1769480 | tf_op jit(solution)/shard_map/ppermute | solution.py:43
  222.3 23.7 %collective-permute-start.21 = (bf16[4,24,3072]{2,1,0:T(8,128)(2,1)}, bf16[4,24,3072]{2,1,0:T(8,128)(2,1)}, u32[]{:S(2)}, u32[]{:S(2)}) collective-permute-start(bf16[4,24,3072]{2,1,0:T(8,128)(2,1)} %get-tuple-element.126), channel_id=1, source_target_pairs={{0,4},{1,5},{2,6},{3,7},{4,0},{5,1},{6,2},{7,3},{8,12},{9,13},{10,... | collective-permute-start | bytes 1769480 | tf_op jit(solution)/shard_map/ppermute | solution.py:43
  222.6 23.4 %collective-permute-start.22 = (bf16[4,24,3072]{2,1,0:T(8,128)(2,1)}, bf16[4,24,3072]{2,1,0:T(8,128)(2,1)}, u32[]{:S(2)}, u32[]{:S(2)}) collective-permute-start(bf16[4,24,3072]{2,1,0:T(8,128)(2,1)} %get-tuple-element.127), channel_id=1, source_target_pairs={{0,1},{1,0},{2,3},{3,2},{4,5},{5,4},{6,7},{7,6},{8,9},{9,8},{10,11... | collective-permute-start | bytes 1769480 | tf_op jit(solution)/shard_map/ppermute | solution.py:43
  228.6 30.5 %collective-permute-start.25 = (bf16[16,24,768]{2,1,0:T(8,128)(2,1)S(1)}, bf16[16,24,768]{2,1,0:T(8,128)(2,1)S(1)}, u32[]{:S(2)}, u32[]{:S(2)}) collective-permute-start(bf16[16,24,768]{2,1,0:T(8,128)(2,1)S(1)} %bitcast.194), channel_id=1, source_target_pairs={{0,2},{1,3},{2,0},{3,1},{4,6},{5,7},{6,4},{7,5},{8,10},{9,11},{10,... | collective-permute-start | bytes 1769480 | tf_op jit(solution)/shard_map/ppermute | solution.py:43
  270.5 18.5 %collective-permute-start.26 = (bf16[16,104,768]{2,1,0:T(8,128)(2,1)}, bf16[16,104,768]{2,1,0:T(8,128)(2,1)}, u32[]{:S(2)}, u32[]{:S(2)}) collective-permute-start(bf16[16,104,768]{2,1,0:T(8,128)(2,1)} %bitcast.40), channel_id=1, source_target_pairs={{0,2},{1,3},{2,0},{3,1},{4,6},{5,7},{6,4},{7,5},{8,10},{9,11},{10,... | collective-permute-start | bytes 7667720 | tf_op jit(solution)/shard_map/ppermute | solution.py:43
  278.6 25.8 %collective-permute-start.30 = (bf16[4,24,3072]{2,1,0:T(8,128)(2,1)S(1)}, bf16[4,24,3072]{2,1,0:T(8,128)(2,1)S(1)}, u32[]{:S(2)}, u32[]{:S(2)}) collective-permute-start(bf16[4,24,3072]{2,1,0:T(8,128)(2,1)S(1)} %get-tuple-element.138), channel_id=1, source_target_pairs={{0,4},{1,5},{2,6},{3,7},{4,0},{5,1},{6,2},{7,3},{8,12},{9,13},{10,... | collective-permute-start | bytes 1769480 | tf_op jit(solution)/shard_map/ppermute | solution.py:43
  278.9 25.5 %collective-permute-start.31 = (bf16[4,24,3072]{2,1,0:T(8,128)(2,1)S(1)}, bf16[4,24,3072]{2,1,0:T(8,128)(2,1)S(1)}, u32[]{:S(2)}, u32[]{:S(2)}) collective-permute-start(bf16[4,24,3072]{2,1,0:T(8,128)(2,1)S(1)} %get-tuple-element.139), channel_id=1, source_target_pairs={{0,1},{1,0},{2,3},{3,2},{4,5},{5,4},{6,7},{7,6},{8,9},{9,8},{10,11... | collective-permute-start | bytes 1769480 | tf_op jit(solution)/shard_map/ppermute | solution.py:43
  292.4 17.7 %collective-permute-start.29 = (bf16[4,104,768]{2,1,0:T(8,128)(2,1)S(1)}, bf16[4,104,768]{2,1,0:T(8,128)(2,1)S(1)}, u32[]{:S(2)}, u32[]{:S(2)}) collective-permute-start(bf16[4,104,768]{2,1,0:T(8,128)(2,1)S(1)} %get-tuple-element.144), channel_id=1, source_target_pairs={{0,4},{1,5},{2,6},{3,7},{4,0},{5,1},{6,2},{7,3},{8,12},{9,13},{10,... | collective-permute-start | bytes 1916936 | tf_op jit(solution)/shard_map/ppermute | solution.py:43
  293.7 16.3 %collective-permute-start.32 = (bf16[4,104,768]{2,1,0:T(8,128)(2,1)S(1)}, bf16[4,104,768]{2,1,0:T(8,128)(2,1)S(1)}, u32[]{:S(2)}, u32[]{:S(2)}) collective-permute-start(bf16[4,104,768]{2,1,0:T(8,128)(2,1)S(1)} %get-tuple-element.146), channel_id=1, source_target_pairs={{0,1},{1,0},{2,3},{3,2},{4,5},{5,4},{6,7},{7,6},{8,9},{9,8},{10,11... | collective-permute-start | bytes 1916936 | tf_op jit(solution)/shard_map/ppermute | solution.py:43
  307.8 44.4 %collective-permute-start.35 = (bf16[2,24,3072]{2,1,0:T(8,128)(2,1)S(1)}, bf16[2,24,3072]{2,1,0:T(8,128)(2,1)S(1)}, u32[]{:S(2)}, u32[]{:S(2)}) collective-permute-start(bf16[2,24,3072]{2,1,0:T(8,128)(2,1)S(1)} %get-tuple-element.149), channel_id=1, source_target_pairs={{0,1},{1,0},{2,3},{3,2},{4,5},{5,4},{6,7},{7,6},{8,9},{9,8},{10,11... | collective-permute-start | bytes 884744 | tf_op jit(solution)/shard_map/ppermute | solution.py:43
  314.4 32.5 %collective-permute-start.37 = (bf16[2,104,768]{2,1,0:T(8,128)(2,1)S(1)}, bf16[2,104,768]{2,1,0:T(8,128)(2,1)S(1)}, u32[]{:S(2)}, u32[]{:S(2)}) collective-permute-start(bf16[2,104,768]{2,1,0:T(8,128)(2,1)S(1)} %get-tuple-element.152), channel_id=1, source_target_pairs={{0,1},{1,0},{2,3},{3,2},{4,5},{5,4},{6,7},{7,6},{8,9},{9,8},{10,11... | collective-permute-start | bytes 958472 | tf_op jit(solution)/shard_map/ppermute | solution.py:43
  315.5 12.5 %collective-permute-start.33 = (bf16[2,104,768]{2,1,0:T(8,128)(2,1)S(1)}, bf16[2,104,768]{2,1,0:T(8,128)(2,1)S(1)}, u32[]{:S(2)}, u32[]{:S(2)}) collective-permute-start(bf16[2,104,768]{2,1,0:T(8,128)(2,1)S(1)} %get-tuple-element.153), channel_id=1, source_target_pairs={{0,4},{1,5},{2,6},{3,7},{4,0},{5,1},{6,2},{7,3},{8,12},{9,13},{10,... | collective-permute-start | bytes 958472 | tf_op jit(solution)/shard_map/ppermute | solution.py:43
  323.1 29.1 %collective-permute-start.36 = (bf16[2,24,3072]{2,1,0:T(8,128)(2,1)S(1)}, bf16[2,24,3072]{2,1,0:T(8,128)(2,1)S(1)}, u32[]{:S(2)}, u32[]{:S(2)}) collective-permute-start(bf16[2,24,3072]{2,1,0:T(8,128)(2,1)S(1)} %add_z.4), channel_id=1, source_target_pairs={{0,8},{1,9},{2,10},{3,11},{4,12},{5,13},{6,14},{7,15},{8,0},{9,1},... | collective-permute-start | bytes 884744 | tf_op jit(solution)/shard_map/ppermute | solution.py:43
  330.2 16.7 %collective-permute-start.38 = (bf16[2,104,768]{2,1,0:T(8,128)(2,1)S(1)}, bf16[2,104,768]{2,1,0:T(8,128)(2,1)S(1)}, u32[]{:S(2)}, u32[]{:S(2)}) collective-permute-start(bf16[2,104,768]{2,1,0:T(8,128)(2,1)S(1)} %add_z.5), channel_id=1, source_target_pairs={{0,8},{1,9},{2,10},{3,11},{4,12},{5,13},{6,14},{7,15},{8,0},{9,1},... | collective-permute-start | bytes 958472 | tf_op jit(solution)/shard_map/ppermute | solution.py:43
  366.5 21.0 %collective-permute-start.48 = (bf16[1,24,3072]{2,1,0:T(8,128)(2,1)S(1)}, bf16[1,24,3072]{2,1,0:T(8,128)(2,1)S(1)}, u32[]{:S(2)}, u32[]{:S(2)}) collective-permute-start(bf16[1,24,3072]{2,1,0:T(8,128)(2,1)S(1)} %add_far.3), channel_id=1, source_target_pairs={{0,16},{1,17},{2,18},{3,19},{4,20},{5,21},{6,22},{7,23},{8,24},{9,... | collective-permute-start | bytes 442376 | tf_op jit(solution)/shard_map/ppermute | solution.py:43
  366.5 23.7 %collective-permute-start.47 = (bf16[1,24,3072]{2,1,0:T(8,128)(2,1)S(1)}, bf16[1,24,3072]{2,1,0:T(8,128)(2,1)S(1)}, u32[]{:S(2)}, u32[]{:S(2)}) collective-permute-start(bf16[1,24,3072]{2,1,0:T(8,128)(2,1)S(1)} %add_far.5), channel_id=1, source_target_pairs={{0,16},{1,17},{2,18},{3,19},{4,20},{5,21},{6,22},{7,23},{8,24},{9,... | collective-permute-start | bytes 442376 | tf_op jit(solution)/shard_map/ppermute | solution.py:43
  381.8 13.3 %collective-permute-start.46 = (f32[40,768]{1,0:T(8,128)S(1)}, f32[40,768]{1,0:T(8,128)}, u32[]{:S(2)}, u32[]{:S(2)}) collective-permute-start(f32[40,768]{1,0:T(8,128)S(1)} %add_add_fusion.2), channel_id=1, source_target_pairs={{0,24},{1,25},{2,26},{3,27},{4,28},{5,29},{6,30},{7,31},{8,16},{9,... | collective-permute-start | bytes 368648 | tf_op jit(solution)/shard_map/ppermute | solution.py:43
  (116 other events, 745.0 us)
Sparse Core Ops, SparseCore 0:
  14.7 103.2 all-gather.2
  270.9 122.5 reduce-scatter.1
